TPU v7x, 32 devices: a whole 2x2x4 slice. The times are simulated.
32 devices in a mesh: tm: 4 (over x, core), height: 8 (over z, y).
Axes of the slice: x: 2, y: 2, z: 4, core: 2. Of those that a mesh axis runs over, the one named last changes fastest.
Arguments:
- queries: bfloat16 [16, 64, 4, 1536], P('tm', 'height'), may hold values from -6 to 6
- key_tokens: bfloat16 [16, 64, 4, 1536], P('tm', 'height'), may hold values from -6 to 6
- value_tokens: bfloat16 [16, 64, 4, 1536], P('tm', 'height'), may hold values from -6 to 6
- out_weight: bfloat16 [1536, 3072], P('height'), may hold values from -0.15625 to 0.15625
- out_grad: bfloat16 [16, 64, 4, 3072], P('tm', 'height'), may hold values from -6 to 6
- window_reach: int32 [4, 8, 2], replicated, may hold values from 0 to 2, as said below
- tile_valid: int32 [4, 8], replicated, may hold values 0 or 1
Outputs:
- attn_out: bfloat16 [16, 64, 4, 3072], P('tm', 'height')
- grad_query: bfloat16 [16, 64, 4, 1536], P('tm', 'height')
- grad_key: bfloat16 [16, 64, 4, 1536], P('tm', 'height')
- grad_value: bfloat16 [16, 64, 4, 1536], P('tm', 'height')
- grad_weight: float32 [1536, 3072], P('height', 'tm')
Inputs may be any that keep to these rules, and one draw needn't show every extreme that they name: `window_reach`: entry 0 is a tile's reach in frames and entry 1 its reach in rows; some tile reaches 2 in both.
All inputs are finite; a program needn't handle non-finite values.
Results may differ from a plain program's by a relative error of at most 0.014.
Values may be sent and summed in bfloat16 or wider, within the bound.
A program may use at most 128 MiB of HBM per device.

v0:
```python
import math

import jax
import jax.numpy as jnp
from jax import lax
from jax.sharding import PartitionSpec as P

HEAD_DIM = 128
HALO = 2


def padded(shard, sides, width):
    for axis, dim in sides:
        count, length = (lax.axis_size(axis), shard.shape[dim])
        up = [(i, (i + 1) % count) for i in range(count - 1)]
        down = [(j, i) for i, j in up]
        last = lax.slice_in_dim(shard, length - width, length, axis=dim)
        first = lax.slice_in_dim(shard, 0, width, axis=dim)
        before = lax.ppermute(last, axis, up)
        after = lax.ppermute(first, axis, down)
        shard = jnp.concatenate([before, shard, after], axis=dim)
    return shard


def passed_along(value, axis, steps):
    count = lax.axis_size(axis)
    first, last = (max(0, -steps), min(count, count - steps))
    return lax.ppermute(value, axis, [(source, source + steps) for source in range(first, last)])


def key_mask(
    window_reach, tile_valid, frame_tile, row_tile, tile_frames, tile_rows, margin, columns
):
    tiles_frames = tile_valid.shape[0]
    tiles_rows = tile_valid.shape[1]
    ext_frames = tile_frames + 2 * margin
    ext_rows = tile_rows + 2 * margin
    frame_pos = jnp.arange(ext_frames, dtype=jnp.int32)
    row_pos = jnp.arange(ext_rows, dtype=jnp.int32)
    frame_ids = jnp.arange(tiles_frames, dtype=jnp.int32)
    row_ids = jnp.arange(tiles_rows, dtype=jnp.int32)
    marked = (frame_ids[:, None] == frame_tile) & (row_ids[None, :] == row_tile)
    reach_frame = jnp.sum(jnp.where(marked, window_reach[:, :, 0], 0))
    reach_row = jnp.sum(jnp.where(marked, window_reach[:, :, 1], 0))
    global_frame = frame_tile * tile_frames - margin + frame_pos
    global_row = row_tile * tile_rows - margin + row_pos
    own_frame = (frame_pos >= margin) & (frame_pos < margin + tile_frames)
    own_row = (row_pos >= margin) & (row_pos < margin + tile_rows)
    near_frame = (frame_pos >= margin - reach_frame) & (
        frame_pos < margin + tile_frames + reach_frame
    )
    near_frame = near_frame & (global_frame >= 0) & (global_frame < tiles_frames * tile_frames)
    near_row = (row_pos >= margin - reach_row) & (row_pos < margin + tile_rows + reach_row)
    near_row = near_row & (global_row >= 0) & (global_row < tiles_rows * tile_rows)
    onehot_frame = (
        jnp.floor_divide(global_frame, tile_frames)[:, None] == frame_ids[None, :]
    ).astype(jnp.float32)
    onehot_row = (jnp.floor_divide(global_row, tile_rows)[:, None] == row_ids[None, :]).astype(
        jnp.float32
    )
    valid = jnp.dot(jnp.dot(onehot_frame, tile_valid.astype(jnp.float32)), onehot_row.T) > 0.5
    allowed = (
        own_frame[:, None] & own_row[None, :] | near_frame[:, None] & near_row[None, :] & valid
    )
    return jnp.broadcast_to(allowed[:, :, None], (ext_frames, ext_rows, columns)).reshape(-1)


def attend(tile_queries, ext_keys, ext_values, d_mixed, allowed):
    score_scale = 1.0 / math.sqrt(HEAD_DIM)
    scores = (
        jnp.einsum("qhd,khd->hqk", tile_queries, ext_keys, preferred_element_type=jnp.float32)
        * score_scale
    )
    scores = jnp.where(allowed[None, None, :], scores, -1e30)
    row_max = jnp.max(scores, axis=-1, keepdims=True)
    expo = jnp.exp(scores - row_max)
    prob = expo / jnp.sum(expo, axis=-1, keepdims=True)
    probs = prob.astype(jnp.bfloat16)
    mixed = jnp.einsum(
        "hqk,khd->qhd", probs, ext_values, preferred_element_type=jnp.float32
    ).astype(jnp.bfloat16)
    d_probs = jnp.einsum("qhd,khd->hqk", d_mixed, ext_values, preferred_element_type=jnp.float32)
    inner = jnp.sum(prob * d_probs, axis=-1, keepdims=True)
    d_scores = (prob * (d_probs - inner) * score_scale).astype(jnp.bfloat16)
    d_query = jnp.einsum(
        "hqk,khd->qhd", d_scores, ext_keys, preferred_element_type=jnp.float32
    ).astype(jnp.bfloat16)
    d_key = jnp.einsum("hqk,qhd->khd", d_scores, tile_queries, preferred_element_type=jnp.float32)
    d_value = jnp.einsum("hqk,qhd->khd", probs, d_mixed, preferred_element_type=jnp.float32)
    return (mixed, d_query, d_key, d_value)


def shards(queries, key_tokens, value_tokens, out_weight, out_grad, window_reach, tile_valid):
    tile_frames, tile_rows, columns, width = queries.shape
    model_width = out_grad.shape[3]
    tokens = tile_frames * tile_rows * columns
    heads = width // HEAD_DIM
    margin = HALO
    ext_frames = tile_frames + 2 * margin
    ext_rows = tile_rows + 2 * margin
    ext_count = ext_frames * ext_rows * columns
    full_weight = lax.all_gather(out_weight, "height", axis=0, tiled=True)
    grad_rows = out_grad.reshape(tokens, model_width)
    d_mixed = lax.dot_general(
        grad_rows, full_weight, (((1,), (1,)), ((), ())), preferred_element_type=jnp.float32
    ).astype(jnp.bfloat16)
    stacked = jnp.stack([key_tokens, value_tokens], axis=3)
    extended = padded(stacked, (("tm", 0), ("height", 1)), margin)
    ext_keys = extended[:, :, :, 0, :].reshape(ext_count, heads, HEAD_DIM)
    ext_values = extended[:, :, :, 1, :].reshape(ext_count, heads, HEAD_DIM)
    frame_tile = lax.axis_index("tm")
    row_tile = lax.axis_index("height")
    allowed = key_mask(
        window_reach, tile_valid, frame_tile, row_tile, tile_frames, tile_rows, margin, columns
    )
    mixed, d_query, d_key, d_value = attend(
        queries.reshape(tokens, heads, HEAD_DIM),
        ext_keys,
        ext_values,
        d_mixed.reshape(tokens, heads, HEAD_DIM),
        allowed,
    )
    mixed_rows = mixed.reshape(tokens, width)
    attn_out = jnp.dot(mixed_rows, full_weight, preferred_element_type=jnp.float32).astype(
        jnp.bfloat16
    )
    attn_out = attn_out.reshape(tile_frames, tile_rows, columns, model_width)
    row_share = lax.psum_scatter(
        lax.dot_general(
            mixed_rows, grad_rows, (((0,), (0,)), ((), ())), preferred_element_type=jnp.float32
        ).astype(jnp.bfloat16),
        "height",
        scatter_dimension=0,
        tiled=True,
    )
    grad_weight = lax.psum_scatter(row_share, "tm", scatter_dimension=1, tiled=True).astype(
        jnp.float32
    )
    key_value_grads = jnp.stack(
        [d_key.reshape(ext_count, width), d_value.reshape(ext_count, width)], axis=1
    )
    key_value_grads = key_value_grads.reshape(ext_frames, ext_rows, columns, 2, width)
    upper_rows = key_value_grads[:, :margin]
    lower_rows = key_value_grads[:, margin + tile_rows :]
    middle_rows = key_value_grads[:, margin : margin + tile_rows]
    from_next_row = passed_along(upper_rows.astype(jnp.bfloat16), "height", -1).astype(
        upper_rows.dtype
    )
    from_prev_row = passed_along(lower_rows.astype(jnp.bfloat16), "height", 1).astype(
        lower_rows.dtype
    )
    middle_rows = jnp.concatenate(
        [
            middle_rows[:, :margin] + from_prev_row,
            middle_rows[:, margin : tile_rows - margin],
            middle_rows[:, tile_rows - margin :] + from_next_row,
        ],
        axis=1,
    )
    upper_frames = middle_rows[:margin]
    lower_frames = middle_rows[margin + tile_frames :]
    middle_frames = middle_rows[margin : margin + tile_frames]
    from_next_frame = passed_along(upper_frames.astype(jnp.bfloat16), "tm", -1).astype(
        upper_frames.dtype
    )
    from_prev_frame = passed_along(lower_frames.astype(jnp.bfloat16), "tm", 1).astype(
        lower_frames.dtype
    )
    own_grads = jnp.concatenate(
        [
            middle_frames[:margin] + from_prev_frame,
            middle_frames[margin : tile_frames - margin],
            middle_frames[tile_frames - margin :] + from_next_frame,
        ],
        axis=0,
    )
    grad_query = d_query.reshape(tile_frames, tile_rows, columns, width)
    grad_key = own_grads[:, :, :, 0, :].astype(jnp.bfloat16)
    grad_value = own_grads[:, :, :, 1, :].astype(jnp.bfloat16)
    return (attn_out, grad_query, grad_key, grad_value, grad_weight)


def solution(mesh):
    return jax.shard_map(
        shards,
        mesh=mesh,
        in_specs=(
            P("tm", "height", None, None),
            P("tm", "height", None, None),
            P("tm", "height", None, None),
            P("height", None),
            P("tm", "height", None, None),
            P(),
            P(),
        ),
        out_specs=(
            P("tm", "height", None, None),
            P("tm", "height", None, None),
            P("tm", "height", None, None),
            P("tm", "height", None, None),
            P("height", "tm"),
        ),
        check_vma=False,
    )
```

profile of v0, /device:TPU:0, one launch (start us, length us, event | category | flops | bytes accessed | tf_op | source)
XLA Modules:
  0.0 367.9 jit_solution(9377724077778961661)
XLA Ops:
  11.2 3.1 collective-permute-start
  21.5 6.3 %collective-permute-start.2 = (bf16[8,2,4,2,1536]{4,2,1,0,3:T(4,128)(2,1)}, bf16[8,2,4,2,1536]{4,2,1,0,3:T(4,128)(2,1)}, u32[]{:S(2)}, u32[]{:S(2)}) collective-permute-start(bf16[8,2,4,2,1536]{4,2,1,0,3:T(4,128)(2,1)} %get-tuple-element.22), channel_id=1, source_target_pairs={{0,1},{1,2},{2,3},{3,4},{4,5},{5,6},{6,7},{8,9},{9,10},{10,11},{11... | collective-permute-start | bytes 1179656 | tf_op jit(solution)/shard_map/ppermute | solution.py:19
  29.2 14.2 %collective-permute-done.3 = bf16[8,2,4,2,1536]{4,2,1,0,3:T(4,128)(2,1)S(1)} collective-permute-done((bf16[8,2,4,2,1536]{4,2,1,0,3:T(4,128)(2,1)}, bf16[8,2,4,2,1536]{4,2,1,0,3:T(4,128)(2,1)S(1)}, u32[]{:S(2)}, u32[]{:S(2)}) %collective-permute-start.3) | collective-permute-done | bytes 393248 | tf_op jit(solution)/shard_map/ppermute | solution.py:20
  43.4 6.6 %collective-permute-done.2 = bf16[8,2,4,2,1536]{4,2,1,0,3:T(4,128)(2,1)} collective-permute-done((bf16[8,2,4,2,1536]{4,2,1,0,3:T(4,128)(2,1)}, bf16[8,2,4,2,1536]{4,2,1,0,3:T(4,128)(2,1)}, u32[]{:S(2)}, u32[]{:S(2)}) %collective-permute-start.2) | collective-permute-done | bytes 393248 | tf_op jit(solution)/shard_map/ppermute | solution.py:19
  50.0 3.2 pad_maximum_fusion.1
  62.1 5.0 %convolution_convert_fusion = bf16[1536,3072]{1,0:T(8,128)(2,1)} fusion(bf16[128,1536]{0,1:T(8,128)(2,1)S(1)} %bitcast.51, bf16[128,3072]{1,0:T(8,128)(2,1)S(1)} %reshape.129), kind=kOutput, calls=%fused_computation.2 | convolution fusion | flops 1212678144 | bytes 10616832 | tf_op jit(solution)/shard_map/dot_general | solution.py:129
  67.3 91.7 %all-gather.2.cloned.1.call-done = bf16[1536,3072]{1,0:T(8,128)(2,1)} async-done(((bf16[192,3072]{1,0:T(8,128)(2,1)}), bf16[1536,3072]{1,0:T(8,128)(2,1)}) %all-gather.2.cloned.1.call-update) | async-done | bytes 9437200 | tf_op jit(solution)/shard_map/all_gather | solution.py:102
  159.0 6.9 %convolution_convert_fusion.2 = bf16[128,1536]{1,0:T(8,128)(2,1)S(1)} fusion(bf16[128,3072]{1,0:T(8,128)(2,1)S(1)} %reshape.129, bf16[1536,3072]{1,0:T(8,128)(2,1)} %all-gather.2.cloned.1.call-done), kind=kOutput, calls=%fused_computation.5 | convolution fusion | flops 1208156160 | bytes 10616832 | tf_op jit(solution)/shard_map/dot_general | solution.py:104
  168.1 6.3 %fusion.15 = f32[384,12,128]{2,0,1:T(8,128)} fusion(f32[12,128,384]{1,2,0:T(8,128)} %fusion.42, bf16[128,12,128]{2,1,0:T(8,128)(2,1)S(1)} %copy-done.4, f32[12,128,384]{1,2,0:T(8,128)} %copy-done.9, f32[12,128]{1,0:T(8,128)S(1)} %get-tuple-element.30), kind=kOutput, calls=%fused_computation.18 | convolution fusion | flops 155125632 | bytes 7477248 | tf_op jit(solution)/shard_map/hqk,qhd->khd/dot_general | solution.py:88
  174.4 3.1 copy.39
  179.4 3.8 %convolution_bitcast_fusion = f32[384,12,128]{0,2,1:T(8,128)} fusion(bf16[128,12,128]{0,2,1:T(8,128)(2,1)} %bitcast.54, f32[12,128,384]{1,2,0:T(8,128)} %copy-done.9, f32[12,128]{1,0:T(8,128)S(1)} %get-tuple-element.30), kind=kOutput, calls=%fused_computation.17 | convolution fusion | flops 152174592 | bytes 5117952 | tf_op jit(solution)/shard_map/hqk,qhd->khd/dot_general | solution.py:89
  183.2 2.6 copy.41
  187.8 2.1 constant_dynamic-update-slice_fusion.1
  189.9 2.1 constant_dynamic-update-slice_fusion
  193.5 3.1 collective-permute-start.4
  198.0 2.3 convolution_convert_fusion.1
  200.3 13.5 %collective-permute-done.4 = bf16[8,2,4,2,1536]{4,2,1,0,3:T(4,128)(2,1)S(1)} collective-permute-done((bf16[8,2,4,2,1536]{4,2,1,0,3:T(4,128)(2,1)S(1)}, bf16[8,2,4,2,1536]{4,2,1,0,3:T(4,128)(2,1)S(1)}, u32[]{:S(2)}, u32[]{:S(2)}) %collective-permute-start.4) | collective-permute-done | bytes 393248 | tf_op jit(solution)/shard_map/ppermute | solution.py:28
  213.8 2.4 collective-permute-done.5
  216.7 115.4 %reduce-scatter.3.cloned.1.call-done = bf16[192,3072]{1,0:T(8,128)(2,1)} async-done(((bf16[1536,3072]{1,0:T(8,128)(2,1)}), bf16[192,3072]{1,0:T(8,128)(2,1)}) %reduce-scatter.3.cloned.1.call-update) | async-done | bytes 1179664 | tf_op jit(solution)/shard_map/reduce_scatter | solution.py:128
  337.6 6.4 %fusion.21 = bf16[128,12,128]{0,2,1:T(8,128)(2,1)} fusion(bf16[384,12,128]{0,2,1:T(8,128)(2,1)} %copy-done.1, f32[12,128,384]{1,2,0:T(8,128)} %fusion.42, f32[12,128,384]{1,2,0:T(8,128)} %copy-done.9, f32[12,128]{1,0:T(8,128)S(1)} %get-tuple-element.30), kind=kOutput, calls=%fused_computation.22 | convolution fusion | flops 155322240 | bytes 6297600 | tf_op jit(solution)/shard_map/hqk,khd->qhd/dot_general | solution.py:85
  344.0 2.4 reshape.128
  346.4 2.2 copy.37
  348.5 2.0 reshape.131
  354.5 5.0 %reduce-scatter.5.cloned.1.call-done = bf16[192,768]{1,0:T(8,128)(2,1)} async-done(((bf16[192,3072]{1,0:T(8,128)(2,1)}), bf16[192,768]{1,0:T(8,128)(2,1)}) %reduce-scatter.5.cloned.1.call-update) | async-done | bytes 294928 | tf_op jit(solution)/shard_map/reduce_scatter | solution.py:136
  (79 shorter events, 39.4 us)
Async XLA Ops:
  7.2 11.5 %copy-start.2 = (bf16[4,8,4,1536]{3,2,1,0:T(4,128)(2,1)S(1)}, bf16[4,8,4,1536]{3,2,1,0:T(4,128)(2,1)}, u32[]{:S(2)}) copy-start(bf16[4,8,4,1536]{3,2,1,0:T(4,128)(2,1)} %param.8) | copy-start | bytes 1179652
  7.2 11.5 %copy-start.3 = (bf16[4,8,4,1536]{3,2,1,0:T(4,128)(2,1)S(1)}, bf16[4,8,4,1536]{3,2,1,0:T(4,128)(2,1)}, u32[]{:S(2)}) copy-start(bf16[4,8,4,1536]{3,2,1,0:T(4,128)(2,1)} %param.9) | copy-start | bytes 1179652
  7.2 7.1 %copy-start.8 = (s32[4,8,2]{1,2,0:T(2,128)S(1)}, s32[4,8,2]{1,2,0:T(2,128)}, u32[]{:S(2)}) copy-start(s32[4,8,2]{1,2,0:T(2,128)} %param.12) | copy-start | bytes 772
  7.2 7.1 %copy-start.7 = (bf16[4,8,4,1536]{3,2,1,0:T(4,128)(2,1)S(1)}, bf16[4,8,4,1536]{3,2,1,0:T(4,128)(2,1)}, u32[]{:S(2)}) copy-start(bf16[4,8,4,1536]{3,2,1,0:T(4,128)(2,1)} %param.7) | copy-start | bytes 1179652
  7.2 151.8 %all-gather.2.cloned.1.call-start = ((), (), s32[]{:S(2)}) async-start(), calls=%async_computation.2 | async-start | bytes 10616832 | tf_op jit(solution)/shard_map/all_gather | solution.py:102
  7.9 324.2 %reduce-scatter.3.cloned.1.call-start = ((), (), s32[]{:S(2)}) async-start(), calls=%async_computation.3 | async-start | bytes 10616832 | tf_op jit(solution)/shard_map/reduce_scatter | solution.py:128
  8.0 21.0 %copy-start.6 = (bf16[4,8,4,3072]{3,2,1,0:T(4,128)(2,1)S(1)}, bf16[4,8,4,3072]{3,2,1,0:T(4,128)(2,1)}, u32[]{:S(2)}) copy-start(bf16[4,8,4,3072]{3,2,1,0:T(4,128)(2,1)} %param.11) | copy-start | bytes 2359300
  9.9 8.8 %collective-permute-start.1 = (bf16[2,8,4,2,1536]{4,2,1,0,3:T(4,128)(2,1)S(1)}, bf16[2,8,4,2,1536]{4,2,1,0,3:T(4,128)(2,1)S(1)}, u32[]{:S(2)}, u32[]{:S(2)}) collective-permute-start(bf16[2,8,4,2,1536]{4,2,1,0,3:T(4,128)(2,1)S(1)} %get-tuple-element.27), channel_id=1, source_target_pairs={{8,0},{16,8},{24,16},{9,1},{17,9},{25,17},{10,2},{18,10},{26,18},{... | collective-permute-start | bytes 1179656 | tf_op jit(solution)/shard_map/ppermute | solution.py:20
  11.2 7.5 %collective-permute-start = (bf16[2,8,4,2,1536]{4,2,1,0,3:T(4,128)(2,1)S(1)}, bf16[2,8,4,2,1536]{4,2,1,0,3:T(4,128)(2,1)S(1)}, u32[]{:S(2)}, u32[]{:S(2)}) collective-permute-start(bf16[2,8,4,2,1536]{4,2,1,0,3:T(4,128)(2,1)S(1)} %get-tuple-element.26), channel_id=1, source_target_pairs={{0,8},{8,16},{16,24},{1,9},{9,17},{17,25},{2,10},{10,18},{18,26},{... | collective-permute-start | bytes 1179656 | tf_op jit(solution)/shard_map/ppermute | solution.py:19
  20.2 23.2 %collective-permute-start.3 = (bf16[8,2,4,2,1536]{4,2,1,0,3:T(4,128)(2,1)}, bf16[8,2,4,2,1536]{4,2,1,0,3:T(4,128)(2,1)S(1)}, u32[]{:S(2)}, u32[]{:S(2)}) collective-permute-start(bf16[8,2,4,2,1536]{4,2,1,0,3:T(4,128)(2,1)} %get-tuple-element.23), channel_id=1, source_target_pairs={{1,0},{2,1},{3,2},{4,3},{5,4},{6,5},{7,6},{9,8},{10,9},{11,10},{12... | collective-permute-start | bytes 1179656 | tf_op jit(solution)/shard_map/ppermute | solution.py:20
  21.5 28.5 %collective-permute-start.2 = (bf16[8,2,4,2,1536]{4,2,1,0,3:T(4,128)(2,1)}, bf16[8,2,4,2,1536]{4,2,1,0,3:T(4,128)(2,1)}, u32[]{:S(2)}, u32[]{:S(2)}) collective-permute-start(bf16[8,2,4,2,1536]{4,2,1,0,3:T(4,128)(2,1)} %get-tuple-element.22), channel_id=1, source_target_pairs={{0,1},{1,2},{2,3},{3,4},{4,5},{5,6},{6,7},{8,9},{9,10},{10,11},{11... | collective-permute-start | bytes 1179656 | tf_op jit(solution)/shard_map/ppermute | solution.py:19
  57.8 2.8 copy-start.1
  59.8 1.4 copy-start
  60.7 1.4 copy-start.9
  67.1 292.4 %reduce-scatter.5.cloned.1.call-start = ((), (), s32[]{:S(2)}) async-start(), calls=%async_computation.4 | async-start | bytes 1474560 | tf_op jit(solution)/shard_map/reduce_scatter | solution.py:136
  165.9 2.2 copy-start.4
  166.2 1.9 copy-start.5
  187.8 10.2 %slice-start = ((s8[9437184]{0:T(1024)(128)(4,1)}), s8[4194304]{0:T(1024)(128)(4,1)S(1)}, s32[]{:S(2)}) async-start(s8[9437184]{0:T(1024)(128)(4,1)} %bitcast.43), calls=%async_computation.5 | async-start | bytes 8388608
  189.9 8.0 %slice-start.1 = ((s8[9437184]{0:T(1024)(128)(4,1)}), s8[4194304]{0:T(1024)(128)(4,1)S(1)}, s32[]{:S(2)}) async-start(s8[9437184]{0:T(1024)(128)(4,1)} %bitcast.43), calls=%async_computation.6 | async-start | bytes 8388608
  192.0 5.9 %slice-start.2 = ((s8[9437184]{0:T(1024)(128)(4,1)}), s8[1048576]{0:T(1024)(128)(4,1)S(1)}, s32[]{:S(2)}) async-start(s8[9437184]{0:T(1024)(128)(4,1)} %bitcast.43), calls=%async_computation.7 | async-start | bytes 2097152
  193.5 20.3 %collective-permute-start.4 = (bf16[8,2,4,2,1536]{4,2,1,0,3:T(4,128)(2,1)S(1)}, bf16[8,2,4,2,1536]{4,2,1,0,3:T(4,128)(2,1)S(1)}, u32[]{:S(2)}, u32[]{:S(2)}) collective-permute-start(bf16[8,2,4,2,1536]{4,2,1,0,3:T(4,128)(2,1)S(1)} %get-tuple-element.16), channel_id=1, source_target_pairs={{0,1},{1,2},{2,3},{3,4},{4,5},{5,6},{6,7},{8,9},{9,10},{10,11},{11... | collective-permute-start | bytes 1179656 | tf_op jit(solution)/shard_map/ppermute | solution.py:28
  196.6 19.6 %collective-permute-start.5 = (bf16[8,2,4,2,1536]{4,2,1,0,3:T(4,128)(2,1)S(1)}, bf16[8,2,4,2,1536]{4,2,1,0,3:T(4,128)(2,1)S(1)}, u32[]{:S(2)}, u32[]{:S(2)}) collective-permute-start(bf16[8,2,4,2,1536]{4,2,1,0,3:T(4,128)(2,1)S(1)} %get-tuple-element.17), channel_id=1, source_target_pairs={{1,0},{2,1},{3,2},{4,3},{5,4},{6,5},{7,6},{9,8},{10,9},{11,10},{12... | collective-permute-start | bytes 1179656 | tf_op jit(solution)/shard_map/ppermute | solution.py:28
  334.3 17.0 %collective-permute-start.6 = (bf16[2,8,4,2,1536]{4,2,1,0,3:T(4,128)(2,1)}, bf16[2,8,4,2,1536]{4,2,1,0,3:T(4,128)(2,1)S(1)}, u32[]{:S(2)}, u32[]{:S(2)}) collective-permute-start(bf16[2,8,4,2,1536]{4,2,1,0,3:T(4,128)(2,1)} %get-tuple-element.20), channel_id=1, source_target_pairs={{0,8},{8,16},{16,24},{1,9},{9,17},{17,25},{2,10},{10,18},{18,26},{... | collective-permute-start | bytes 1179656 | tf_op jit(solution)/shard_map/ppermute | solution.py:28
  336.1 15.2 %collective-permute-start.7 = (bf16[2,8,4,2,1536]{4,2,1,0,3:T(4,128)(2,1)}, bf16[2,8,4,2,1536]{4,2,1,0,3:T(4,128)(2,1)}, u32[]{:S(2)}, u32[]{:S(2)}) collective-permute-start(bf16[2,8,4,2,1536]{4,2,1,0,3:T(4,128)(2,1)} %get-tuple-element.21), channel_id=1, source_target_pairs={{8,0},{16,8},{24,16},{9,1},{17,9},{25,17},{10,2},{18,10},{26,18},{... | collective-permute-start | bytes 1179656 | tf_op jit(solution)/shard_map/ppermute | solution.py:28
Sparse Core Ops, SparseCore 0:
  10.2 148.7 all-gather.1
  162.6 169.4 reduce-scatter.2
  334.7 24.8 reduce-scatter.4
where the time goes:
time: 369 us; the launch traced here: 368 us
  waiting for transfers between devices  250 us (68%)
  matrix products  36.3 us (10%)
  local copies, waits for them, and re-layouts  30.1 us (8%)
  starting transfers between devices  19.9 us (5%)
  between operations  16.8 us (5%)
  other arithmetic  15.2 us (4%)
    reduce_scatter x1, waiting for transfers between devices, shards(): lax.psum_scatter(lax.dot_general(mixed_rows, grad_rows, (((0,), (0,)), ((...  115 us
    all_gather x1, waiting for transfers between devices, shards(): full_weight = lax.all_gather(out_weight, 'height', axis=0, tiled=True)  91.7 us
    ppermute x4, waiting for transfers between devices, passed_along(): lax.ppermute(value, axis, [(source, source + steps) for source in range(f...  15.9 us
    ppermute x2, waiting for transfers between devices, padded(): after = lax.ppermute(first, axis, down)  14.2 us
    ppermute x2, starting transfers between devices, padded(): before = lax.ppermute(last, axis, up)  9.32 us
    ppermute x4, starting transfers between devices, passed_along(): lax.ppermute(value, axis, [(source, source + steps) for source in range(f...  7.74 us
  transfers between devices with their start and end apart: 11, of which 7 were waited for; matrix products, arithmetic and copies ran while one was open for 21% of the time, Pallas kernels for 0%

commit v1 on v0

v1 whole, which is shorter than its diff:
```python
import functools
import math

import jax
import jax.numpy as jnp
import numpy as np
from jax import lax
from jax.experimental import pallas as pl
from jax.experimental.pallas import tpu as pltpu
from jax.sharding import PartitionSpec as P

HEAD_DIM = 128
HALO = 2
MESH = pl.DeviceIdType.MESH
F32 = jnp.float32
BF16 = jnp.bfloat16
SIDES = ((-1, 0), (1, 0), (0, -1), (0, 1), (-1, -1), (-1, 1), (1, -1), (1, 1))


def piece_sizes(frames, rows, columns):
    sizes = []
    for df, dr in SIDES:
        sizes.append((HALO if df else frames) * (HALO if dr else rows) * columns)
    return sizes


def key_bias(window_reach, tile_valid, t, h, frames, rows, columns):
    tables = []
    for df, dr in ((0, 0),) + SIDES:
        fs = range(HALO) if df else range(frames)
        rs = range(HALO) if dr else range(rows)
        for f in fs:
            for r in rs:
                fd = 0 if df == 0 else (HALO - f if df < 0 else f + 1)
                rd = 0 if dr == 0 else (HALO - r if dr < 0 else r + 1)
                tables += [(df, dr, fd, rd)] * columns
    table = np.array(tables, np.int32)
    df, dr, fd, rd = (jnp.asarray(table[:, i]) for i in range(4))
    nt, nh = tile_valid.shape
    ti = jnp.arange(nt, dtype=jnp.int32)[:, None]
    hi = jnp.arange(nh, dtype=jnp.int32)[None, :]
    mine = ((ti == t) & (hi == h)).astype(jnp.int32)
    reach = jnp.sum(window_reach * mine[:, :, None], axis=(0, 1))
    hit = (ti[None] == (t + df)[:, None, None]) & (hi[None] == (h + dr)[:, None, None])
    valid = jnp.sum(jnp.where(hit, tile_valid[None], 0), axis=(1, 2)) > 0
    own = (df == 0) & (dr == 0)
    allowed = own | ((fd <= reach[0]) & (rd <= reach[1]) & valid)
    return jnp.where(allowed, 0.0, -1e30).astype(F32)[None, :]


def piece_rows(df, dr, frames, rows, columns):
    fs = range(frames) if df == 0 else (range(frames - HALO, frames) if df < 0 else range(HALO))
    if dr == 0:
        return [(fs[0] * rows * columns, len(fs) * rows * columns)]
    first = (rows - HALO) if dr < 0 else 0
    return [((f * rows + first) * columns, HALO * columns) for f in fs]


def kernel(
    dims,
    q_ref, k_ref, v_ref, bias_ref, w_hbm, og_hbm,
    attn_ref, dq_ref, dk_ref, dv_ref, gw_ref,
    wfull, ogfull, kvsend, kvext, gsend, grecv, prob, dmixed, mixed, mixwin, acc, gwin,
    local_sem, halo_s, halo_r, grad_s, grad_r, mix_s, mix_r,
    wr_s, wr_r, wl_s, wl_r, wc_s, wc_r, or_s, or_r, ol_s, ol_r,
):
    nt, nh, frames, rows, columns = dims
    t, h = lax.axis_index("tm"), lax.axis_index("height")
    tokens, width = q_ref.shape
    model = og_hbm.shape[1]
    share = w_hbm.shape[0]
    heads = width // HEAD_DIM
    half = model // 2
    window = mixwin.shape[1]
    scale = 1.0 / math.sqrt(HEAD_DIM)
    sizes = piece_sizes(frames, rows, columns)
    starts = [sum(sizes[:i]) for i in range(8)]

    def place(df, dr):
        return (lax.rem(t + nt + df, nt), lax.rem(h + nh + dr, nh))

    def remote(src, dst, ssem, rsem, where):
        return pltpu.make_async_remote_copy(
            src_ref=src, dst_ref=dst, send_sem=ssem, recv_sem=rsem,
            device_id=where, device_id_type=MESH,
        )

    def wrow(j, lo=0, size=None):
        return pl.ds(pl.multiple_of(j * share + lo, 16), share if size is None else size)

    def orow(j, lo=0, size=None):
        return pl.ds(pl.multiple_of(j * tokens + lo, 16), tokens if size is None else size)

    own_w = pltpu.make_async_copy(w_hbm, wfull.at[wrow(h), :], local_sem.at[0])
    own_og = pltpu.make_async_copy(og_hbm, ogfull.at[orow(h), :], local_sem.at[1])
    own_w.start()
    own_og.start()

    barrier = pltpu.get_barrier_semaphore()
    greeted = 0
    for i in range(1, nh):
        pl.semaphore_signal(barrier, inc=1, device_id=(t, lax.rem(h + i, nh)), device_id_type=MESH)
        greeted += 1
    for df, dr in SIDES:
        if df:
            pl.semaphore_signal(barrier, inc=1, device_id=place(df, dr), device_id_type=MESH)
            greeted += 1

    for i, ref in enumerate((k_ref, v_ref)):
        x = ref[...]
        kvext[i, 0:tokens, :] = x
        x = x.astype(F32)
        for s, (df, dr) in enumerate(SIDES):
            parts = [x[a : a + n] for a, n in piece_rows(df, dr, frames, rows, columns)]
            y = parts[0] if len(parts) == 1 else jnp.concatenate(parts, axis=0)
            kvsend[i, starts[s] : starts[s] + sizes[s], :] = y.astype(BF16)

    pl.semaphore_wait(barrier, greeted)
    halos = []
    for s, (df, dr) in enumerate(SIDES):
        copy = remote(
            kvsend.at[:, pl.ds(starts[s], sizes[s]), :],
            kvext.at[:, pl.ds(tokens + starts[s], sizes[s]), :],
            halo_s.at[s], halo_r.at[s], place(-df, -dr),
        )
        copy.start()
        halos.append(copy)

    par = lax.rem(h, 2)
    pos = (1 - par) * (h // 2) + par * (nh - 1 - h // 2)

    def at(p):
        p = lax.rem(p + nh, nh)
        far = p // (nh // 2)
        return (1 - far) * (2 * p) + far * (2 * (nh - 1 - p) + 1)

    right, left = (t, at(pos + 1)), (t, at(pos - 1))
    steps = nh // 2
    core = lax.rem(t, 2)
    partner = (t + 1 - 2 * core, h)
    mine = pl.ds(pl.multiple_of(core * half, 128), half)

    def span(step, size, side):
        if step < steps - 1:
            return 0, size
        return (0 if side == 0 else size // 2), size // 2

    def ring_sends(step, buf, rowfn, size, cols, sems):
        out = []
        for side, (target, sign) in enumerate(((right, -1), (left, 1))):
            lo, n = span(step, size, side)
            ref = buf.at[rowfn(at(pos + sign * step), lo, n), cols]
            ssem, rsem = sems[2 * side], sems[2 * side + 1]
            copy = remote(ref, ref, ssem.at[step], rsem.at[step], target)
            copy.start()
            out.append(copy)
        return out

    wsems = (wr_s, wr_r, wl_s, wl_r)
    osems = (or_s, or_r, ol_s, ol_r)
    allcols = pl.ds(0, model)

    def w_sends(step):
        return ring_sends(step, wfull, wrow, share, mine, wsems)

    def og_sends(step):
        return ring_sends(step, ogfull, orow, tokens, allcols, osems)

    def core_sends(step):
        out = []
        for side, sign in enumerate((-1, 1)):
            lo, n = span(step, share, side)
            ref = wfull.at[wrow(at(pos + sign * (step + 1)), lo, n), mine]
            copy = remote(ref, ref, wc_s.at[2 * step + side], wc_r.at[2 * step + side], partner)
            copy.start()
            out.append(copy)
        return out

    own_w.wait()
    own_og.wait()
    w_copies = w_sends(0)
    core_copies = []
    w_live = list(w_copies)

    for copy in halos:
        copy.wait()

    group = 3 if heads % 3 == 0 else 1

    def cols_of(c):
        return pl.ds(pl.multiple_of(c * HEAD_DIM, HEAD_DIM), HEAD_DIM)

    def nt_dot(a, b):
        return lax.dot_general(a, b, (((1,), (1,)), ((), ())), preferred_element_type=F32)

    def tn_dot(a, b):
        return lax.dot_general(a, b, (((0,), (0,)), ((), ())), preferred_element_type=F32)

    def nn_dot(a, b):
        return lax.dot_general(a, b, (((1,), (0,)), ((), ())), preferred_element_type=F32)

    def forward(g, carry):
        for j in range(group):
            c = g * group + j
            cs = cols_of(c)
            scores = nt_dot(q_ref[:, cs], kvext[0, :, cs]) * scale + bias_ref[...]
            e = jnp.exp(scores - jnp.max(scores, axis=-1, keepdims=True))
            p = e / jnp.sum(e, axis=-1, keepdims=True)
            prob[c] = p
            mixed[:, cs] = nn_dot(p.astype(BF16), kvext[1, :, cs]).astype(BF16)
        return carry

    lax.fori_loop(0, heads // group, forward, 0)

    def window_start(j):
        block = (j * share) // 128
        last = (width - window) // 128
        block = jnp.minimum(block, last)
        return pl.multiple_of(block * 128, 128)

    mixwin[orow(h), :] = mixed[:, pl.ds(window_start(h), window)]
    mix_copies = []
    for i in range(1, nh):
        j = lax.rem(h + i, nh)
        copy = remote(
            mixed.at[:, pl.ds(window_start(j), window)], mixwin.at[orow(h), :],
            mix_s.at[i - 1], mix_r.at[i - 1], (t, j),
        )
        copy.start()
        mix_copies.append(copy)

    og_live = []
    for step in range(steps):
        for copy in w_live:
            copy.wait()
        w_live = []
        if step < steps - 1:
            w_live = w_sends(step + 1)
        else:
            og_live = og_sends(0)
        core_copies += core_sends(step)
    for copy in core_copies:
        copy.wait()

    def project(i, carry):
        r = pl.ds(pl.multiple_of(i * 256, 256), 256)
        dmixed[:, r] = nt_dot(ogfull[orow(h), :], wfull[r, :]).astype(BF16)
        return carry

    lax.fori_loop(0, width // 256, project, 0)

    def backward(g, carry):
        for j in range(group):
            c = g * group + j
            cs = cols_of(c)
            p = prob[c]
            dm = dmixed[:, cs]
            dp = nt_dot(dm, kvext[1, :, cs])
            inner = jnp.sum(p * dp, axis=-1, keepdims=True)
            ds = (p * (dp - inner) * scale).astype(BF16)
            dq_ref[:, cs] = nn_dot(ds, kvext[0, :, cs]).astype(BF16)
            dk = tn_dot(ds, q_ref[:, cs])
            dv = tn_dot(p.astype(BF16), dm)
            acc[0, :, cs] = dk[:tokens]
            acc[1, :, cs] = dv[:tokens]
            gsend[0, :, cs] = dk[tokens:].astype(BF16)
            gsend[1, :, cs] = dv[tokens:].astype(BF16)
        return carry

    lax.fori_loop(0, heads // group, backward, 0)

    grads = []
    for s, (df, dr) in enumerate(SIDES):
        rs = pl.ds(starts[s], sizes[s])
        copy = remote(
            gsend.at[:, rs, :], grecv.at[:, rs, :], grad_s.at[s], grad_r.at[s], place(df, dr)
        )
        copy.start()
        grads.append(copy)

    def og_step(step):
        for copy in og_live:
            copy.wait()
        og_live.clear()
        if step < steps:
            og_live.extend(og_sends(step))

    og_step(1)

    def attn(i, carry):
        cs = pl.ds(pl.multiple_of(i * 256, 256), 256)
        attn_ref[:, cs] = nn_dot(mixed[...], wfull[:, cs]).astype(BF16)
        return carry

    lax.fori_loop(0, model // 256, attn, 0)

    for copy in grads:
        copy.wait()
    for i, ref in enumerate((dk_ref, dv_ref)):
        for s, (df, dr) in enumerate(SIDES):
            y = grecv[i, starts[s] : starts[s] + sizes[s], :].astype(F32)
            first = 0
            for a, n in piece_rows(df, dr, frames, rows, columns):
                acc[i, a : a + n, :] += y[first : first + n]
                first += n
        ref[...] = acc[i].astype(BF16)

    for step in range(2, steps + 1):
        og_step(step)
    for copy in mix_copies:
        copy.wait()

    offset = pl.multiple_of(h * share - window_start(h), 16)

    def weight(i, carry):
        cs = pl.ds(pl.multiple_of(i * 512, 512), 512)
        gwin[...] = tn_dot(mixwin[...], ogfull[:, cs])
        gw_ref[:, cs] = gwin[pl.ds(offset, share), :].astype(BF16)
        return carry

    lax.fori_loop(0, model // 512, weight, 0)


def shards(nt, nh, queries, key_tokens, value_tokens, out_weight, out_grad, window_reach, tile_valid):
    frames, rows, columns, width = queries.shape
    model = out_grad.shape[3]
    share = out_weight.shape[0]
    tokens = frames * rows * columns
    heads = width // HEAD_DIM
    halo = sum(piece_sizes(frames, rows, columns))
    ext = tokens + halo
    window = 256
    t, h = lax.axis_index("tm"), lax.axis_index("height")
    bias = key_bias(window_reach, tile_valid, t, h, frames, rows, columns)
    steps = nh // 2
    vmem = pl.BlockSpec(memory_space=pltpu.VMEM)
    hbm = pl.BlockSpec(memory_space=pl.ANY)
    dma = pltpu.SemaphoreType.DMA
    attn, dq, dk, dv, gw = pl.pallas_call(
        functools.partial(kernel, (nt, nh, frames, rows, columns)),
        out_shape=(
            jax.ShapeDtypeStruct((tokens, model), BF16),
            jax.ShapeDtypeStruct((tokens, width), BF16),
            jax.ShapeDtypeStruct((tokens, width), BF16),
            jax.ShapeDtypeStruct((tokens, width), BF16),
            jax.ShapeDtypeStruct((share, model), BF16),
        ),
        in_specs=[vmem, vmem, vmem, vmem, hbm, hbm],
        out_specs=[vmem] * 5,
        scratch_shapes=[
            pltpu.VMEM((width, model), BF16),
            pltpu.VMEM((nh * tokens, model), BF16),
            pltpu.VMEM((2, halo, width), BF16),
            pltpu.VMEM((2, ext, width), BF16),
            pltpu.VMEM((2, halo, width), BF16),
            pltpu.VMEM((2, halo, width), BF16),
            pltpu.VMEM((heads, tokens, ext), F32),
            pltpu.VMEM((tokens, width), BF16),
            pltpu.VMEM((tokens, width), BF16),
            pltpu.VMEM((nh * tokens, window), BF16),
            pltpu.VMEM((2, tokens, width), F32),
            pltpu.VMEM((window, 512), F32),
            dma((2,)), dma((8,)), dma((8,)), dma((8,)), dma((8,)),
            dma((nh - 1,)), dma((nh - 1,)),
            dma((steps,)), dma((steps,)), dma((steps,)), dma((steps,)),
            dma((2 * steps,)), dma((2 * steps,)),
            dma((steps,)), dma((steps,)), dma((steps,)), dma((steps,)),
        ],
        compiler_params=pltpu.CompilerParams(
            collective_id=0, has_side_effects=True, vmem_limit_bytes=56 * 2**20
        ),
    )(
        queries.reshape(tokens, width),
        key_tokens.reshape(tokens, width),
        value_tokens.reshape(tokens, width),
        bias,
        out_weight,
        out_grad.reshape(tokens, model),
    )
    grad_weight = lax.psum_scatter(gw, "tm", scatter_dimension=1, tiled=True).astype(F32)
    tile = (frames, rows, columns)
    return (
        attn.reshape(*tile, model),
        dq.reshape(*tile, width),
        dk.reshape(*tile, width),
        dv.reshape(*tile, width),
        grad_weight,
    )


def solution(mesh):
    tile = P("tm", "height", None, None)
    return jax.shard_map(
        functools.partial(shards, mesh.shape["tm"], mesh.shape["height"]),
        mesh=mesh,
        in_specs=(tile, tile, tile, P("height", None), tile, P(), P()),
        out_specs=(tile, tile, tile, tile, P("height", "tm")),
        check_vma=False,
    )
```

time: 369 us -> 212 us (0.57)
  waiting for transfers between devices: 250 us -> 19.7 us
  Pallas kernels: 0 us -> 160 us
  matrix products: 36.3 us -> 0 us
  starting transfers between devices: 19.9 us -> 0.04 us
  local copies, waits for them, and re-layouts: 30.1 us -> 11.6 us
  other arithmetic: 15.2 us -> 6.87 us
    pallas_call x0 -> x1, Pallas kernels: none -> 160 us  [shards(): pl.pallas_call(functools.partial(kernel, (nt, nh, frames, rows, columns))...]
    reduce_scatter x2 -> x1, waiting for transfers between devices: 120 us -> 19.7 us  [shards(): lax.psum_scatter(gw, 'tm', scatter_dimension=1, tiled=True).astype(F32)]
    all_gather x1 -> x0, waiting for transfers between devices: 91.7 us -> none  [shards(): full_weight = lax.all_gather(out_weight, 'height', axis=0, tiled=True)]
    ppermute x8 -> x0, waiting for transfers between devices: 36.7 us -> none  [the longest x4 15.9 us: passed_along(): lax.ppermute(value, axis, [(source, source + steps) for source in range(f...]
    dot_general x10 -> x0, matrix products: 36.3 us -> none  [the longest x1 6.9 us: shards(): lax.dot_general(grad_rows, full_weight, (((1,), (1,)), ((), ())), preferr...]
    ppermute x8 -> x0, starting transfers between devices: 19.6 us -> none  [the longest x2 9.32 us: padded(): before = lax.ppermute(last, axis, up)]
    another operation x6 -> x0, local copies, waits for them, and re-layouts: 9.75 us -> none  [the longest x3 5.94 us: shards(): jnp.stack([d_key.reshape(ext_count, width), d_value.reshape(ext_count, wi...]
    transpose x2 -> x0, local copies, waits for them, and re-layouts: 5.73 us -> none  [the longest x1 3.08 us: attend(): jnp.einsum('hqk,qhd->khd', d_scores, tile_queries, preferred_element_type...]
  transfers between devices with their start and end apart: 11 -> 1, of which waited for: 7 -> 1; matrix products, arithmetic and copies ran while one was open for 21% -> 2% of each run, Pallas kernels for 0% -> 0%
where the time goes in v1:
time: 212 us
  Pallas kernels  160 us (75%)
  waiting for transfers between devices  19.7 us (9%)
  between operations  14.1 us (7%)
  local copies, waits for them, and re-layouts  11.6 us (5%)
  other arithmetic  6.87 us (3%)
    pallas_call x1, Pallas kernels, shards(): pl.pallas_call(functools.partial(kernel, (nt, nh, frames, rows, columns))...  160 us
    reduce_scatter x1, waiting for transfers between devices, shards(): lax.psum_scatter(gw, 'tm', scatter_dimension=1, tiled=True).astype(F32)  19.7 us
  transfers between devices with their start and end apart: 1, of which 1 were waited for; matrix products, arithmetic and copies ran while one was open for 2% of the time, Pallas kernels for 0%

profile of v1, /device:TPU:0, one launch (start us, length us, event | category | flops | bytes accessed | tf_op | source)
XLA Modules:
  0.0 212.0 jit_solution(13582820719616165756)
XLA Ops:
  7.2 0.0 copy-start.2
  7.2 0.0 reduce-scatter.2.cloned.1.call-start
  7.3 0.1 and_convert_fusion
  7.3 0.8 multiply_reduce_fusion
  8.1 0.6 fusion
  8.7 0.7 broadcast_add_fusion
  9.4 0.7 broadcast_add_fusion.1
  10.1 0.8 select_reduce_fusion
  10.9 2.0 or_select_fusion
  12.9 0.6 broadcast_in_dim.33.bias_ref
  13.5 1.9 reshape.119.q_ref
  15.4 1.8 reshape.120.k_ref
  17.2 0.0 copy-done.2
  17.2 0.8 reshape.121.v_ref
  18.0 1.1 reshape.122.og_hbm
  19.1 159.8 %shard_map.146 = (bf16[128,3072]{1,0:T(8,128)(2,1)}, bf16[128,1536]{1,0:T(8,128)(2,1)}, bf16[128,1536]{1,0:T(8,128)(2,1)}, bf16[128,1536]{1,0:T(8,128)(2,1)}, bf16[192,3072]{1,0:T(8,128)(2,1)}) custom-call(bf16[128,1536]{1,0:T(8,128)(2,1)} %reshape.119.q_ref, bf16[128,1536]{1,0:T(8,128)(2,1)} %reshape.120.k_ref, bf16[128,1536]{1,0:T(8,128)(2,1)} %reshape.121.v_ref, ...), custom_call_target="tpu_custom_call" | custom-call | tf_op jit(solution)/shard_map/pallas_call | solution.py:339
  178.9 0.0 reduce-scatter.2.cloned.1.call-update
  178.9 1.1 copy-done.1
  180.0 1.2 reshape.123
  181.2 0.8 reshape.124
  182.0 0.8 reshape.125
  182.9 0.8 reshape.126
  183.7 19.7 %reduce-scatter.2.cloned.1.call-done = bf16[192,768]{1,0:T(8,128)(2,1)} async-done(((bf16[192,3072]{1,0:T(8,128)(2,1)}), bf16[192,768]{1,0:T(8,128)(2,1)}) %reduce-scatter.2.cloned.1.call-update) | async-done | bytes 294928 | tf_op jit(solution)/shard_map/reduce_scatter | solution.py:380
  203.3 1.8 convert_element_type.11
  (13 shorter events, 0.0 us)
Async XLA Ops:
  7.2 10.0 %copy-start.2 = (bf16[4,8,4,1536]{3,2,1,0:T(4,128)(2,1)S(1)}, bf16[4,8,4,1536]{3,2,1,0:T(4,128)(2,1)}, u32[]{:S(2)}) copy-start(bf16[4,8,4,1536]{3,2,1,0:T(4,128)(2,1)} %param.13) | copy-start | bytes 1179652
  7.2 196.2 %reduce-scatter.2.cloned.1.call-start = ((), (), s32[]{:S(2)}) async-start(), calls=%async_computation.1 | async-start | bytes 1474560 | tf_op jit(solution)/shard_map/reduce_scatter | solution.py:380
  13.5 4.6 %copy-start = (bf16[4,8,4,3072]{3,2,1,0:T(4,128)(2,1)S(1)}, bf16[4,8,4,3072]{3,2,1,0:T(4,128)(2,1)}, u32[]{:S(2)}) copy-start(bf16[4,8,4,3072]{3,2,1,0:T(4,128)(2,1)} %param.15) | copy-start | bytes 2359300
  178.9 1.1 copy-start.1
  178.9 2.3 %copy-start.5 = (bf16[128,1536]{1,0:T(8,128)(2,1)S(1)}, bf16[128,1536]{1,0:T(8,128)(2,1)}, u32[]{:S(2)}) copy-start(bf16[128,1536]{1,0:T(8,128)(2,1)} %get-tuple-element.11) | copy-start | bytes 1179652
  180.0 2.0 copy-start.4
  181.2 1.7 copy-start.3
Sparse Core Ops, SparseCore 0:
  179.0 24.2 reduce-scatter.1

commit v2 on v1

--- a/solution.py
+++ b/solution.py
@@ -24,28 +24,15 @@
     return sizes
 
 
-def key_bias(window_reach, tile_valid, t, h, frames, rows, columns):
-    tables = []
-    for df, dr in ((0, 0),) + SIDES:
-        fs = range(HALO) if df else range(frames)
-        rs = range(HALO) if dr else range(rows)
-        for f in fs:
-            for r in rs:
+def key_table(frames, rows, columns):
+    table = []
+    for piece, (df, dr) in enumerate(((0, 0),) + SIDES):
+        for f in range(HALO) if df else range(frames):
+            for r in range(HALO) if dr else range(rows):
                 fd = 0 if df == 0 else (HALO - f if df < 0 else f + 1)
                 rd = 0 if dr == 0 else (HALO - r if dr < 0 else r + 1)
-                tables += [(df, dr, fd, rd)] * columns
-    table = np.array(tables, np.int32)
-    df, dr, fd, rd = (jnp.asarray(table[:, i]) for i in range(4))
-    nt, nh = tile_valid.shape
-    ti = jnp.arange(nt, dtype=jnp.int32)[:, None]
-    hi = jnp.arange(nh, dtype=jnp.int32)[None, :]
-    mine = ((ti == t) & (hi == h)).astype(jnp.int32)
-    reach = jnp.sum(window_reach * mine[:, :, None], axis=(0, 1))
-    hit = (ti[None] == (t + df)[:, None, None]) & (hi[None] == (h + dr)[:, None, None])
-    valid = jnp.sum(jnp.where(hit, tile_valid[None], 0), axis=(1, 2)) > 0
-    own = (df == 0) & (dr == 0)
-    allowed = own | ((fd <= reach[0]) & (rd <= reach[1]) & valid)
-    return jnp.where(allowed, 0.0, -1e30).astype(F32)[None, :]
+                table += [(piece, fd, rd)] * columns
+    return np.ascontiguousarray(np.array(table, np.int32).T)
 
 
 def piece_rows(df, dr, frames, rows, columns):
@@ -58,11 +45,11 @@
 
 def kernel(
     dims,
-    q_ref, k_ref, v_ref, bias_ref, w_hbm, og_hbm,
+    q_ref, k_ref, v_ref, table_ref, reach_ref, valid_ref, w_hbm, og_hbm,
     attn_ref, dq_ref, dk_ref, dv_ref, gw_ref,
-    wfull, ogfull, kvsend, kvext, gsend, grecv, prob, dmixed, mixed, mixwin, acc, gwin,
+    wfull, ogfull, kvsend, kvext, gsend, grecv, prob, dmixed, mixed, mixwin, acc, gwin, bias_ref, gwsend, gwrecv,
     local_sem, halo_s, halo_r, grad_s, grad_r, mix_s, mix_r,
-    wr_s, wr_r, wl_s, wl_r, wc_s, wc_r, or_s, or_r, ol_s, ol_r,
+    wr_s, wr_r, wl_s, wl_r, wc_s, wc_r, wx_s, wx_r, wf_s, wf_r, or_s, or_r, ol_s, ol_r, gw_s, gw_r,
 ):
     nt, nh, frames, rows, columns = dims
     t, h = lax.axis_index("tm"), lax.axis_index("height")
@@ -70,7 +57,7 @@
     model = og_hbm.shape[1]
     share = w_hbm.shape[0]
     heads = width // HEAD_DIM
-    half = model // 2
+    quarter = model // 4
     window = mixwin.shape[1]
     scale = 1.0 / math.sqrt(HEAD_DIM)
     sizes = piece_sizes(frames, rows, columns)
@@ -78,6 +65,18 @@
 
     def place(df, dr):
         return (lax.rem(t + nt + df, nt), lax.rem(h + nh + dr, nh))
+
+    def exists(df, dr):
+        a, b = t + df, h + dr
+        return (a >= 0) & (a < nt) & (b >= 0) & (b < nh)
+
+    def exchange(copies, sign, action):
+        for (df, dr), copy in zip(SIDES, copies):
+            if action == "start":
+                pl.when(exists(sign * df, sign * dr))(copy.start)
+            else:
+                pl.when(exists(sign * df, sign * dr))(copy.wait_send)
+                pl.when(exists(-sign * df, -sign * dr))(copy.wait_recv)
 
     def remote(src, dst, ssem, rsem, where):
         return pltpu.make_async_remote_copy(
@@ -101,10 +100,22 @@
     for i in range(1, nh):
         pl.semaphore_signal(barrier, inc=1, device_id=(t, lax.rem(h + i, nh)), device_id_type=MESH)
         greeted += 1
+    for i in range(1, nt):
+        pl.semaphore_signal(barrier, inc=1, device_id=(lax.rem(t + i, nt), h), device_id_type=MESH)
+        greeted += 1
     for df, dr in SIDES:
-        if df:
+        if df and dr:
             pl.semaphore_signal(barrier, inc=1, device_id=place(df, dr), device_id_type=MESH)
             greeted += 1
+
+    piece = table_ref[0:1, :]
+    hit = jnp.ones_like(piece)
+    for s, (df, dr) in enumerate(SIDES):
+        a, b = place(df, dr)
+        here = jnp.where(exists(df, dr), valid_ref[a, b], 0)
+        hit = jnp.where(piece == s + 1, here, hit)
+    near = (table_ref[1:2, :] <= reach_ref[t, h, 0]) & (table_ref[2:3, :] <= reach_ref[t, h, 1])
+    bias_ref[...] = jnp.where((piece == 0) | (near & (hit == 1)), 0.0, -1e30)
 
     for i, ref in enumerate((k_ref, v_ref)):
         x = ref[...]
@@ -115,16 +126,12 @@
             y = parts[0] if len(parts) == 1 else jnp.concatenate(parts, axis=0)
             kvsend[i, starts[s] : starts[s] + sizes[s], :] = y.astype(BF16)
 
-    pl.semaphore_wait(barrier, greeted)
-    halos = []
     for s, (df, dr) in enumerate(SIDES):
-        copy = remote(
-            kvsend.at[:, pl.ds(starts[s], sizes[s]), :],
-            kvext.at[:, pl.ds(tokens + starts[s], sizes[s]), :],
-            halo_s.at[s], halo_r.at[s], place(-df, -dr),
-        )
-        copy.start()
-        halos.append(copy)
+
+        @pl.when(jnp.logical_not(exists(df, dr)))
+        def _():
+            rs = pl.ds(tokens + starts[s], sizes[s])
+            kvext[:, rs, :] = jnp.zeros((2, sizes[s], width), BF16)
 
     par = lax.rem(h, 2)
     pos = (1 - par) * (h // 2) + par * (nh - 1 - h // 2)
@@ -138,7 +145,14 @@
     steps = nh // 2
     core = lax.rem(t, 2)
     partner = (t + 1 - 2 * core, h)
-    mine = pl.ds(pl.multiple_of(core * half, 128), half)
+    pair = lax.rem(t // 2, 2)
+    across = (t + 2 - 4 * pair, h)
+
+    def quarter_of(i):
+        return pl.ds(pl.multiple_of(i * quarter, 128), quarter)
+
+    mine = quarter_of(2 * pair + core)
+    theirs = quarter_of(2 * (1 - pair) + core)
 
     def span(step, size, side):
         if step < steps - 1:
@@ -166,24 +180,49 @@
     def og_sends(step):
         return ring_sends(step, ogfull, orow, tokens, allcols, osems)
 
-    def core_sends(step):
+    def share_sends(step):
         out = []
         for side, sign in enumerate((-1, 1)):
             lo, n = span(step, share, side)
             ref = wfull.at[wrow(at(pos + sign * (step + 1)), lo, n), mine]
-            copy = remote(ref, ref, wc_s.at[2 * step + side], wc_r.at[2 * step + side], partner)
+            i = 2 * step + side
+            out.append(remote(ref, ref, wx_s.at[i], wx_r.at[i], across))
+            out.append(remote(ref, ref, wc_s.at[i], wc_r.at[i], partner))
+        for copy in out:
+            copy.start()
+        return out
+
+    def pass_on(step):
+        out = []
+        for side, sign in enumerate((-1, 1)):
+            lo, n = span(step, share, side)
+            ref = wfull.at[wrow(at(pos + sign * (step + 1)), lo, n), theirs]
+            i = 2 * step + side
+            copy = remote(ref, ref, wf_s.at[i], wf_r.at[i], partner)
             copy.start()
             out.append(copy)
         return out
 
     own_w.wait()
     own_og.wait()
-    w_copies = w_sends(0)
-    core_copies = []
-    w_live = list(w_copies)
-
-    for copy in halos:
-        copy.wait()
+    pl.semaphore_wait(barrier, greeted)
+    halos = []
+    for s, (df, dr) in enumerate(SIDES):
+        copy = remote(
+            kvsend.at[:, pl.ds(starts[s], sizes[s]), :],
+            kvext.at[:, pl.ds(tokens + starts[s], sizes[s]), :],
+            halo_s.at[s], halo_r.at[s], place(-df, -dr),
+        )
+        halos.append(copy)
+    exchange(halos, -1, "start")
+    live = w_sends(0)
+    shared = []
+    for step in range(steps):
+        for copy in live:
+            copy.wait()
+        live = w_sends(step + 1) if step < steps - 1 else og_sends(0)
+        shared.append(share_sends(step))
+    exchange(halos, -1, "wait")
 
     group = 3 if heads % 3 == 0 else 1
 
@@ -229,17 +268,21 @@
         copy.start()
         mix_copies.append(copy)
 
-    og_live = []
+    def og_step(step):
+        for copy in live:
+            copy.wait()
+        live.clear()
+        if step < steps:
+            live.extend(og_sends(step))
+
+    passed = []
     for step in range(steps):
-        for copy in w_live:
+        for copy in shared[step]:
             copy.wait()
-        w_live = []
-        if step < steps - 1:
-            w_live = w_sends(step + 1)
-        else:
-            og_live = og_sends(0)
-        core_copies += core_sends(step)
-    for copy in core_copies:
+        passed += pass_on(step)
+        if step == steps // 2:
+            og_step(1)
+    for copy in passed:
         copy.wait()
 
     def project(i, carry):
@@ -248,6 +291,8 @@
         return carry
 
     lax.fori_loop(0, width // 256, project, 0)
+
+    og_step(2)
 
     def backward(g, carry):
         for j in range(group):
@@ -275,17 +320,9 @@
         copy = remote(
             gsend.at[:, rs, :], grecv.at[:, rs, :], grad_s.at[s], grad_r.at[s], place(df, dr)
         )
-        copy.start()
         grads.append(copy)
-
-    def og_step(step):
-        for copy in og_live:
-            copy.wait()
-        og_live.clear()
-        if step < steps:
-            og_live.extend(og_sends(step))
-
-    og_step(1)
+    exchange(grads, 1, "start")
+    og_step(3)
 
     def attn(i, carry):
         cs = pl.ds(pl.multiple_of(i * 256, 256), 256)
@@ -294,31 +331,49 @@
 
     lax.fori_loop(0, model // 256, attn, 0)
 
-    for copy in grads:
-        copy.wait()
+    exchange(grads, 1, "wait")
     for i, ref in enumerate((dk_ref, dv_ref)):
         for s, (df, dr) in enumerate(SIDES):
-            y = grecv[i, starts[s] : starts[s] + sizes[s], :].astype(F32)
-            first = 0
-            for a, n in piece_rows(df, dr, frames, rows, columns):
-                acc[i, a : a + n, :] += y[first : first + n]
-                first += n
+
+            @pl.when(exists(-df, -dr))
+            def _():
+                y = grecv[i, starts[s] : starts[s] + sizes[s], :].astype(F32)
+                first = 0
+                for a, n in piece_rows(df, dr, frames, rows, columns):
+                    acc[i, a : a + n, :] += y[first : first + n]
+                    first += n
+
         ref[...] = acc[i].astype(BF16)
 
-    for step in range(2, steps + 1):
+    for step in range(4, steps + 1):
         og_step(step)
     for copy in mix_copies:
         copy.wait()
 
     offset = pl.multiple_of(h * share - window_start(h), 16)
 
-    def weight(i, carry):
-        cs = pl.ds(pl.multiple_of(i * 512, 512), 512)
+    block = gwin.shape[1]
+
+    def weight(i):
+        cs = pl.ds(pl.multiple_of(i * block, 128), block)
         gwin[...] = tn_dot(mixwin[...], ogfull[:, cs])
-        gw_ref[:, cs] = gwin[pl.ds(offset, share), :].astype(BF16)
-        return carry
-
-    lax.fori_loop(0, model // 512, weight, 0)
+        return gwin[pl.ds(offset, share), :]
+
+    if gw_ref.shape[1] == model:
+        for i in range(model // block):
+            gw_ref[:, i * block : (i + 1) * block] = weight(i).astype(BF16)
+        return
+    terms = []
+    for i in range(1, nt):
+        j = lax.rem(t + i, nt)
+        gwsend[i - 1] = weight(j).astype(BF16)
+        copy = remote(gwsend.at[i - 1], gwrecv.at[i - 1], gw_s.at[i - 1], gw_r.at[i - 1], (j, h))
+        copy.start()
+        terms.append(copy)
+    gw_ref[...] = weight(t)
+    for copy in terms:
+        copy.wait()
+    gw_ref[...] += sum(gwrecv[i].astype(F32) for i in range(nt - 1))
 
 
 def shards(nt, nh, queries, key_tokens, value_tokens, out_weight, out_grad, window_reach, tile_valid):
@@ -330,10 +385,13 @@
     halo = sum(piece_sizes(frames, rows, columns))
     ext = tokens + halo
     window = 256
-    t, h = lax.axis_index("tm"), lax.axis_index("height")
-    bias = key_bias(window_reach, tile_valid, t, h, frames, rows, columns)
+    table = key_table(frames, rows, columns)
+    narrow = (model // nt) % 128 == 0
+    block = model // nt if narrow else 512
+    slots = nt - 1 if narrow else 1
     steps = nh // 2
     vmem = pl.BlockSpec(memory_space=pltpu.VMEM)
+    smem = pl.BlockSpec(memory_space=pltpu.SMEM)
     hbm = pl.BlockSpec(memory_space=pl.ANY)
     dma = pltpu.SemaphoreType.DMA
     attn, dq, dk, dv, gw = pl.pallas_call(
@@ -343,9 +401,11 @@
             jax.ShapeDtypeStruct((tokens, width), BF16),
             jax.ShapeDtypeStruct((tokens, width), BF16),
             jax.ShapeDtypeStruct((tokens, width), BF16),
-            jax.ShapeDtypeStruct((share, model), BF16),
+            jax.ShapeDtypeStruct((share, block), F32)
+            if narrow
+            else jax.ShapeDtypeStruct((share, model), BF16),
         ),
-        in_specs=[vmem, vmem, vmem, vmem, hbm, hbm],
+        in_specs=[vmem, vmem, vmem, vmem, smem, smem, hbm, hbm],
         out_specs=[vmem] * 5,
         scratch_shapes=[
             pltpu.VMEM((width, model), BF16),
@@ -359,12 +419,17 @@
             pltpu.VMEM((tokens, width), BF16),
             pltpu.VMEM((nh * tokens, window), BF16),
             pltpu.VMEM((2, tokens, width), F32),
-            pltpu.VMEM((window, 512), F32),
+            pltpu.VMEM((window, block), F32),
+            pltpu.VMEM((1, ext), F32),
+            pltpu.VMEM((slots, share, block), BF16),
+            pltpu.VMEM((slots, share, block), BF16),
             dma((2,)), dma((8,)), dma((8,)), dma((8,)), dma((8,)),
             dma((nh - 1,)), dma((nh - 1,)),
             dma((steps,)), dma((steps,)), dma((steps,)), dma((steps,)),
+            dma((2 * steps,)), dma((2 * steps,)), dma((2 * steps,)), dma((2 * steps,)),
             dma((2 * steps,)), dma((2 * steps,)),
             dma((steps,)), dma((steps,)), dma((steps,)), dma((steps,)),
+            dma((nt - 1,)), dma((nt - 1,)),
         ],
         compiler_params=pltpu.CompilerParams(
             collective_id=0, has_side_effects=True, vmem_limit_bytes=56 * 2**20
@@ -373,18 +438,21 @@
         queries.reshape(tokens, width),
         key_tokens.reshape(tokens, width),
         value_tokens.reshape(tokens, width),
-        bias,
+        table,
+        window_reach,
+        tile_valid,
         out_weight,
         out_grad.reshape(tokens, model),
     )
-    grad_weight = lax.psum_scatter(gw, "tm", scatter_dimension=1, tiled=True).astype(F32)
+    if not narrow:
+        gw = lax.psum_scatter(gw, "tm", scatter_dimension=1, tiled=True).astype(F32)
     tile = (frames, rows, columns)
     return (
         attn.reshape(*tile, model),
         dq.reshape(*tile, width),
         dk.reshape(*tile, width),
         dv.reshape(*tile, width),
-        grad_weight,
+        gw,
     )
 
 

time: 212 us -> 157 us (0.74); the launches traced: 212 us -> 155 us
  waiting for transfers between devices: 19.7 us -> 0 us
  Pallas kernels: 160 us -> 141 us
  between operations: 14.1 us -> 0.68 us
  other arithmetic: 6.87 us -> 0 us
    reduce_scatter x1 -> x0, waiting for transfers between devices: 19.7 us -> none  [shards(): lax.psum_scatter(gw, 'tm', scatter_dimension=1, tiled=True).astype(F32)]
    pallas_call x1, Pallas kernels: 160 us -> 141 us  [shards(): pl.pallas_call(functools.partial(kernel, (nt, nh, frames, rows, columns))...]
  transfers between devices with their start and end apart: 1 -> 0, of which waited for: 1 -> 0; matrix products, arithmetic and copies ran while one was open for 2% -> 0% of each run, Pallas kernels for 0% -> 0%
where the time goes in v2:
time: 157 us; the launch traced here: 155 us
  Pallas kernels  141 us (90%)
  local copies, waits for them, and re-layouts  12.9 us (8%)
    pallas_call x1, Pallas kernels, shards(): pl.pallas_call(functools.partial(kernel, (nt, nh, frames, rows, columns))...  141 us

profile of v2, /device:TPU:0, one launch (start us, length us, event | category | flops | bytes accessed | tf_op | source)
XLA Modules:
  0.0 154.8 jit_solution(18203407925896501534)
XLA Ops:
  0.6 0.0 copy-start.2
  0.6 1.4 copy.13.reach_ref
  2.1 0.0 copy-start
  2.1 1.9 %reshape.34.q_ref = bf16[128,1536]{1,0:T(8,128)(2,1)} reshape(bf16[4,8,4,1536]{3,2,1,0:T(4,128)(2,1)} %param.8) | data formatting | bytes 786432 | tf_op jit(solution)/shard_map/reshape | solution.py:438
  4.0 1.8 %reshape.35.k_ref = bf16[128,1536]{1,0:T(8,128)(2,1)} reshape(bf16[4,8,4,1536]{3,2,1,0:T(4,128)(2,1)} %param.9) | data formatting | bytes 786432 | tf_op jit(solution)/shard_map/reshape | solution.py:439
  5.8 0.0 copy-done.2
  5.8 0.8 reshape.36.v_ref
  6.7 0.0 copy-done
  6.7 1.1 reshape.37.og_hbm
  7.7 141.3 %shard_map.119 = (bf16[128,3072]{1,0:T(8,128)(2,1)}, bf16[128,1536]{1,0:T(8,128)(2,1)}, bf16[128,1536]{1,0:T(8,128)(2,1)}, bf16[128,1536]{1,0:T(8,128)(2,1)}, f32[192,768]{1,0:T(8,128)}) custom-call(bf16[128,1536]{1,0:T(8,128)(2,1)} %reshape.34.q_ref, bf16[128,1536]{1,0:T(8,128)(2,1)} %reshape.35.k_ref, bf16[128,1536]{1,0:T(8,128)(2,1)} %reshape.36.v_ref, ...), custom_call_target="tpu_custom_call" | custom-call | tf_op jit(solution)/shard_map/pallas_call | solution.py:397
  149.0 0.0 copy-start.5
  149.0 0.0 copy-start.4
  149.0 2.4 %reshape.38 = bf16[4,8,4,3072]{3,2,1,0:T(4,128)(2,1)} reshape(bf16[128,3072]{1,0:T(8,128)(2,1)} %get-tuple-element.10) | data formatting | bytes 1572864 | tf_op jit(solution)/shard_map/reshape | solution.py:451
  151.5 0.0 copy-done.5
  151.5 0.0 copy-start.3
  151.5 0.0 copy-start.1
  151.5 0.8 reshape.39
  152.3 0.0 copy-done.4
  152.3 0.8 reshape.40
  153.2 0.0 copy-done.3
  153.2 0.8 reshape.41
  154.0 0.0 copy-done.1
  154.0 0.8 copy.15
Async XLA Ops:
  0.6 5.2 %copy-start.2 = (bf16[4,8,4,1536]{3,2,1,0:T(4,128)(2,1)S(1)}, bf16[4,8,4,1536]{3,2,1,0:T(4,128)(2,1)}, u32[]{:S(2)}) copy-start(bf16[4,8,4,1536]{3,2,1,0:T(4,128)(2,1)} %param.10) | copy-start | bytes 1179652
  2.1 4.6 %copy-start = (bf16[4,8,4,3072]{3,2,1,0:T(4,128)(2,1)S(1)}, bf16[4,8,4,3072]{3,2,1,0:T(4,128)(2,1)}, u32[]{:S(2)}) copy-start(bf16[4,8,4,3072]{3,2,1,0:T(4,128)(2,1)} %param.12) | copy-start | bytes 2359300
  149.0 2.5 %copy-start.5 = (bf16[128,1536]{1,0:T(8,128)(2,1)S(1)}, bf16[128,1536]{1,0:T(8,128)(2,1)}, u32[]{:S(2)}) copy-start(bf16[128,1536]{1,0:T(8,128)(2,1)} %get-tuple-element.11) | copy-start | bytes 1179652
  149.0 3.3 %copy-start.4 = (bf16[128,1536]{1,0:T(8,128)(2,1)S(1)}, bf16[128,1536]{1,0:T(8,128)(2,1)}, u32[]{:S(2)}) copy-start(bf16[128,1536]{1,0:T(8,128)(2,1)} %get-tuple-element.12) | copy-start | bytes 1179652
  151.5 1.7 %copy-start.3 = (bf16[128,1536]{1,0:T(8,128)(2,1)S(1)}, bf16[128,1536]{1,0:T(8,128)(2,1)}, u32[]{:S(2)}) copy-start(bf16[128,1536]{1,0:T(8,128)(2,1)} %get-tuple-element.13) | copy-start | bytes 1179652
  151.5 2.5 %copy-start.1 = (f32[192,768]{1,0:T(8,128)S(1)}, f32[192,768]{1,0:T(8,128)}, u32[]{:S(2)}) copy-start(f32[192,768]{1,0:T(8,128)} %get-tuple-element.24) | copy-start | bytes 1769476

commit v3 on v2

--- a/solution.py
+++ b/solution.py
@@ -47,9 +47,9 @@
     dims,
     q_ref, k_ref, v_ref, table_ref, reach_ref, valid_ref, w_hbm, og_hbm,
     attn_ref, dq_ref, dk_ref, dv_ref, gw_ref,
-    wfull, ogfull, kvsend, kvext, gsend, grecv, prob, dmixed, mixed, mixwin, acc, gwin, bias_ref, gwsend, gwrecv,
+    wfull, ogown, ogcols, kvsend, kvext, gsend, grecv, prob, dmixed, mixed, mixall, acc, gpart, bias_ref, gwsend, gwrecv,
     local_sem, halo_s, halo_r, grad_s, grad_r, mix_s, mix_r,
-    wr_s, wr_r, wl_s, wl_r, wc_s, wc_r, wx_s, wx_r, wf_s, wf_r, or_s, or_r, ol_s, ol_r, gw_s, gw_r,
+    wr_s, wr_r, wl_s, wl_r, wc_s, wc_r, wx_s, wx_r, wf_s, wf_r, og_s, og_r, gw_s, gw_r,
 ):
     nt, nh, frames, rows, columns = dims
     t, h = lax.axis_index("tm"), lax.axis_index("height")
@@ -58,7 +58,8 @@
     share = w_hbm.shape[0]
     heads = width // HEAD_DIM
     quarter = model // 4
-    window = mixwin.shape[1]
+    window = gpart.shape[1]
+    span_cols = model // nt
     scale = 1.0 / math.sqrt(HEAD_DIM)
     sizes = piece_sizes(frames, rows, columns)
     starts = [sum(sizes[:i]) for i in range(8)]
@@ -91,7 +92,7 @@
         return pl.ds(pl.multiple_of(j * tokens + lo, 16), tokens if size is None else size)
 
     own_w = pltpu.make_async_copy(w_hbm, wfull.at[wrow(h), :], local_sem.at[0])
-    own_og = pltpu.make_async_copy(og_hbm, ogfull.at[orow(h), :], local_sem.at[1])
+    own_og = pltpu.make_async_copy(og_hbm, ogown, local_sem.at[1])
     own_w.start()
     own_og.start()
 
@@ -171,14 +172,35 @@
         return out
 
     wsems = (wr_s, wr_r, wl_s, wl_r)
-    osems = (or_s, or_r, ol_s, ol_r)
-    allcols = pl.ds(0, model)
-
     def w_sends(step):
         return ring_sends(step, wfull, wrow, share, mine, wsems)
 
-    def og_sends(step):
-        return ring_sends(step, ogfull, orow, tokens, allcols, osems)
+    def gw_sends(step):
+        out = []
+        for side, (target, sign) in enumerate(((right, 1), (left, -1))):
+            base = at(pos + sign * (steps - step)) * share
+            cut = share // 2
+            for part in range(2):
+                if step == 0 and part != side:
+                    continue
+                rs = slice(part * cut, (part + 1) * cut)
+                total = gpart[pl.ds(pl.multiple_of(base + part * cut, 16), cut), :]
+                if step > 1 or (step == 1 and part == side):
+                    total += gwrecv[side, step - 1, rs, :].astype(F32)
+                gwsend[side, step, rs, :] = total.astype(BF16)
+            rs = pl.ds(side * cut, cut) if step == 0 else pl.ds(0, share)
+            i = side * steps + step
+            copy = remote(
+                gwsend.at[side, step, rs, :], gwrecv.at[side, step, rs, :],
+                gw_s.at[i], gw_r.at[i], target,
+            )
+            copy.start()
+            out.append(copy)
+        return out
+
+    def cols_start(j):
+        block = jnp.minimum((j * span_cols) // 128, (model - window) // 128)
+        return pl.multiple_of(block * 128, 128)
 
     def share_sends(step):
         out = []
@@ -216,11 +238,21 @@
         halos.append(copy)
     exchange(halos, -1, "start")
     live = w_sends(0)
+    ogcols[orow(t), :] = ogown[:, pl.ds(cols_start(t), window)]
+    gathers = []
+    for i in range(1, nt):
+        j = lax.rem(t + i, nt)
+        copy = remote(
+            ogown.at[:, pl.ds(cols_start(j), window)], ogcols.at[orow(t), :],
+            og_s.at[i - 1], og_r.at[i - 1], (j, h),
+        )
+        copy.start()
+        gathers.append(copy)
     shared = []
     for step in range(steps):
         for copy in live:
             copy.wait()
-        live = w_sends(step + 1) if step < steps - 1 else og_sends(0)
+        live = w_sends(step + 1) if step < steps - 1 else []
         shared.append(share_sends(step))
     exchange(halos, -1, "wait")
 
@@ -251,48 +283,49 @@
 
     lax.fori_loop(0, heads // group, forward, 0)
 
-    def window_start(j):
-        block = (j * share) // 128
-        last = (width - window) // 128
-        block = jnp.minimum(block, last)
-        return pl.multiple_of(block * 128, 128)
-
-    mixwin[orow(h), :] = mixed[:, pl.ds(window_start(h), window)]
-    mix_copies = []
-    for i in range(1, nh):
-        j = lax.rem(h + i, nh)
+    mixall[orow(t), :] = mixed[...]
+    for i in range(1, nt):
         copy = remote(
-            mixed.at[:, pl.ds(window_start(j), window)], mixwin.at[orow(h), :],
-            mix_s.at[i - 1], mix_r.at[i - 1], (t, j),
+            mixed, mixall.at[orow(t), :], mix_s.at[i - 1], mix_r.at[i - 1],
+            (lax.rem(t + i, nt), h),
         )
         copy.start()
-        mix_copies.append(copy)
-
-    def og_step(step):
+        gathers.append(copy)
+
+    def gw_step(step):
         for copy in live:
             copy.wait()
         live.clear()
         if step < steps:
-            live.extend(og_sends(step))
+            live.extend(gw_sends(step))
 
     passed = []
     for step in range(steps):
         for copy in shared[step]:
             copy.wait()
         passed += pass_on(step)
-        if step == steps // 2:
-            og_step(1)
+
+    for copy in gathers:
+        copy.wait()
+
+    def weight(i, carry):
+        cs = pl.ds(pl.multiple_of(i * 256, 256), 256)
+        gpart[cs, :] = tn_dot(mixall[:, cs], ogcols[...])
+        return carry
+
+    lax.fori_loop(0, width // 256, weight, 0)
+    gw_step(0)
     for copy in passed:
         copy.wait()
 
     def project(i, carry):
         r = pl.ds(pl.multiple_of(i * 256, 256), 256)
-        dmixed[:, r] = nt_dot(ogfull[orow(h), :], wfull[r, :]).astype(BF16)
+        dmixed[:, r] = nt_dot(ogown[...], wfull[r, :]).astype(BF16)
         return carry
 
     lax.fori_loop(0, width // 256, project, 0)
 
-    og_step(2)
+    gw_step(1)
 
     def backward(g, carry):
         for j in range(group):
@@ -322,7 +355,7 @@
         )
         grads.append(copy)
     exchange(grads, 1, "start")
-    og_step(3)
+    gw_step(2)
 
     def attn(i, carry):
         cs = pl.ds(pl.multiple_of(i * 256, 256), 256)
@@ -330,6 +363,7 @@
         return carry
 
     lax.fori_loop(0, model // 256, attn, 0)
+    gw_step(3)
 
     exchange(grads, 1, "wait")
     for i, ref in enumerate((dk_ref, dv_ref)):
@@ -346,34 +380,12 @@
         ref[...] = acc[i].astype(BF16)
 
     for step in range(4, steps + 1):
-        og_step(step)
-    for copy in mix_copies:
-        copy.wait()
-
-    offset = pl.multiple_of(h * share - window_start(h), 16)
-
-    block = gwin.shape[1]
-
-    def weight(i):
-        cs = pl.ds(pl.multiple_of(i * block, 128), block)
-        gwin[...] = tn_dot(mixwin[...], ogfull[:, cs])
-        return gwin[pl.ds(offset, share), :]
-
-    if gw_ref.shape[1] == model:
-        for i in range(model // block):
-            gw_ref[:, i * block : (i + 1) * block] = weight(i).astype(BF16)
-        return
-    terms = []
-    for i in range(1, nt):
-        j = lax.rem(t + i, nt)
-        gwsend[i - 1] = weight(j).astype(BF16)
-        copy = remote(gwsend.at[i - 1], gwrecv.at[i - 1], gw_s.at[i - 1], gw_r.at[i - 1], (j, h))
-        copy.start()
-        terms.append(copy)
-    gw_ref[...] = weight(t)
-    for copy in terms:
-        copy.wait()
-    gw_ref[...] += sum(gwrecv[i].astype(F32) for i in range(nt - 1))
+        gw_step(step)
+    gw_ref[...] = (
+        gpart[wrow(h), :]
+        + gwrecv[0, steps - 1].astype(F32)
+        + gwrecv[1, steps - 1].astype(F32)
+    )
 
 
 def shards(nt, nh, queries, key_tokens, value_tokens, out_weight, out_grad, window_reach, tile_valid):
@@ -384,11 +396,9 @@
     heads = width // HEAD_DIM
     halo = sum(piece_sizes(frames, rows, columns))
     ext = tokens + halo
-    window = 256
     table = key_table(frames, rows, columns)
     narrow = (model // nt) % 128 == 0
-    block = model // nt if narrow else 512
-    slots = nt - 1 if narrow else 1
+    block = model // nt if narrow else 256
     steps = nh // 2
     vmem = pl.BlockSpec(memory_space=pltpu.VMEM)
     smem = pl.BlockSpec(memory_space=pltpu.SMEM)
@@ -401,15 +411,14 @@
             jax.ShapeDtypeStruct((tokens, width), BF16),
             jax.ShapeDtypeStruct((tokens, width), BF16),
             jax.ShapeDtypeStruct((tokens, width), BF16),
-            jax.ShapeDtypeStruct((share, block), F32)
-            if narrow
-            else jax.ShapeDtypeStruct((share, model), BF16),
+            jax.ShapeDtypeStruct((share, block), F32),
         ),
         in_specs=[vmem, vmem, vmem, vmem, smem, smem, hbm, hbm],
         out_specs=[vmem] * 5,
         scratch_shapes=[
             pltpu.VMEM((width, model), BF16),
-            pltpu.VMEM((nh * tokens, model), BF16),
+            pltpu.VMEM((tokens, model), BF16),
+            pltpu.VMEM((nt * tokens, block), BF16),
             pltpu.VMEM((2, halo, width), BF16),
             pltpu.VMEM((2, ext, width), BF16),
             pltpu.VMEM((2, halo, width), BF16),
@@ -417,19 +426,18 @@
             pltpu.VMEM((heads, tokens, ext), F32),
             pltpu.VMEM((tokens, width), BF16),
             pltpu.VMEM((tokens, width), BF16),
-            pltpu.VMEM((nh * tokens, window), BF16),
+            pltpu.VMEM((nt * tokens, width), BF16),
             pltpu.VMEM((2, tokens, width), F32),
-            pltpu.VMEM((window, block), F32),
+            pltpu.VMEM((width, block), F32),
             pltpu.VMEM((1, ext), F32),
-            pltpu.VMEM((slots, share, block), BF16),
-            pltpu.VMEM((slots, share, block), BF16),
+            pltpu.VMEM((2, steps, share, block), BF16),
+            pltpu.VMEM((2, steps, share, block), BF16),
             dma((2,)), dma((8,)), dma((8,)), dma((8,)), dma((8,)),
-            dma((nh - 1,)), dma((nh - 1,)),
+            dma((nt - 1,)), dma((nt - 1,)),
             dma((steps,)), dma((steps,)), dma((steps,)), dma((steps,)),
             dma((2 * steps,)), dma((2 * steps,)), dma((2 * steps,)), dma((2 * steps,)),
             dma((2 * steps,)), dma((2 * steps,)),
-            dma((steps,)), dma((steps,)), dma((steps,)), dma((steps,)),
-            dma((nt - 1,)), dma((nt - 1,)),
+            dma((nt - 1,)), dma((nt - 1,)), dma((2 * steps,)), dma((2 * steps,)),
         ],
         compiler_params=pltpu.CompilerParams(
             collective_id=0, has_side_effects=True, vmem_limit_bytes=56 * 2**20
@@ -445,7 +453,10 @@
         out_grad.reshape(tokens, model),
     )
     if not narrow:
-        gw = lax.psum_scatter(gw, "tm", scatter_dimension=1, tiled=True).astype(F32)
+        size = model // nt
+        at = lax.axis_index("tm") * size
+        first = jnp.minimum(at // 128, (model - block) // 128) * 128
+        gw = lax.dynamic_slice_in_dim(gw, at - first, size, axis=1)
     tile = (frames, rows, columns)
     return (
         attn.reshape(*tile, model),

time: 157 us -> 153 us (0.975)
  Pallas kernels: 141 us -> 139 us
    pallas_call x1, Pallas kernels: 141 us -> 139 us  [shards(): pl.pallas_call(functools.partial(kernel, (nt, nh, frames, rows, columns))...]
where the time goes in v3:
time: 153 us; the launch traced here: 152 us
  Pallas kernels  139 us (91%)
  local copies, waits for them, and re-layouts  12.9 us (8%)
    pallas_call x1, Pallas kernels, shards(): pl.pallas_call(functools.partial(kernel, (nt, nh, frames, rows, columns))...  139 us

profile of v3, /device:TPU:0, one launch (start us, length us, event | category | flops | bytes accessed | tf_op | source)
XLA Modules:
  0.0 152.3 jit_solution(2149702331981463927)
XLA Ops:
  0.6 0.0 copy-start.2
  0.6 1.4 copy.13.reach_ref
  2.1 0.0 copy-start
  2.1 1.9 %reshape.34.q_ref = bf16[128,1536]{1,0:T(8,128)(2,1)} reshape(bf16[4,8,4,1536]{3,2,1,0:T(4,128)(2,1)} %param.8) | data formatting | bytes 786432 | tf_op jit(solution)/shard_map/reshape | solution.py:446
  4.0 1.8 %reshape.35.k_ref = bf16[128,1536]{1,0:T(8,128)(2,1)} reshape(bf16[4,8,4,1536]{3,2,1,0:T(4,128)(2,1)} %param.9) | data formatting | bytes 786432 | tf_op jit(solution)/shard_map/reshape | solution.py:447
  5.8 0.0 copy-done.2
  5.8 0.8 reshape.36.v_ref
  6.7 0.0 copy-done
  6.7 1.1 reshape.37.og_hbm
  7.7 138.8 %shard_map.119 = (bf16[128,3072]{1,0:T(8,128)(2,1)}, bf16[128,1536]{1,0:T(8,128)(2,1)}, bf16[128,1536]{1,0:T(8,128)(2,1)}, bf16[128,1536]{1,0:T(8,128)(2,1)}, f32[192,768]{1,0:T(8,128)}) custom-call(bf16[128,1536]{1,0:T(8,128)(2,1)} %reshape.34.q_ref, bf16[128,1536]{1,0:T(8,128)(2,1)} %reshape.35.k_ref, bf16[128,1536]{1,0:T(8,128)(2,1)} %reshape.36.v_ref, ...), custom_call_target="tpu_custom_call" | custom-call | tf_op jit(solution)/shard_map/pallas_call | solution.py:407
  146.5 0.0 copy-start.5
  146.5 0.0 copy-start.4
  146.5 2.4 %reshape.38 = bf16[4,8,4,3072]{3,2,1,0:T(4,128)(2,1)} reshape(bf16[128,3072]{1,0:T(8,128)(2,1)} %get-tuple-element.10) | data formatting | bytes 1572864 | tf_op jit(solution)/shard_map/reshape | solution.py:462
  149.0 0.0 copy-done.5
  149.0 0.0 copy-start.3
  149.0 0.0 copy-start.1
  149.0 0.8 reshape.39
  149.8 0.0 copy-done.4
  149.8 0.8 reshape.40
  150.7 0.0 copy-done.3
  150.7 0.8 reshape.41
  151.5 0.0 copy-done.1
  151.5 0.8 copy.15
Async XLA Ops:
  0.6 5.2 %copy-start.2 = (bf16[4,8,4,1536]{3,2,1,0:T(4,128)(2,1)S(1)}, bf16[4,8,4,1536]{3,2,1,0:T(4,128)(2,1)}, u32[]{:S(2)}) copy-start(bf16[4,8,4,1536]{3,2,1,0:T(4,128)(2,1)} %param.10) | copy-start | bytes 1179652
  2.1 4.6 %copy-start = (bf16[4,8,4,3072]{3,2,1,0:T(4,128)(2,1)S(1)}, bf16[4,8,4,3072]{3,2,1,0:T(4,128)(2,1)}, u32[]{:S(2)}) copy-start(bf16[4,8,4,3072]{3,2,1,0:T(4,128)(2,1)} %param.12) | copy-start | bytes 2359300
  146.5 2.5 %copy-start.5 = (bf16[128,1536]{1,0:T(8,128)(2,1)S(1)}, bf16[128,1536]{1,0:T(8,128)(2,1)}, u32[]{:S(2)}) copy-start(bf16[128,1536]{1,0:T(8,128)(2,1)} %get-tuple-element.11) | copy-start | bytes 1179652
  146.5 3.3 %copy-start.4 = (bf16[128,1536]{1,0:T(8,128)(2,1)S(1)}, bf16[128,1536]{1,0:T(8,128)(2,1)}, u32[]{:S(2)}) copy-start(bf16[128,1536]{1,0:T(8,128)(2,1)} %get-tuple-element.12) | copy-start | bytes 1179652
  149.0 1.7 %copy-start.3 = (bf16[128,1536]{1,0:T(8,128)(2,1)S(1)}, bf16[128,1536]{1,0:T(8,128)(2,1)}, u32[]{:S(2)}) copy-start(bf16[128,1536]{1,0:T(8,128)(2,1)} %get-tuple-element.13) | copy-start | bytes 1179652
  149.0 2.5 %copy-start.1 = (f32[192,768]{1,0:T(8,128)S(1)}, f32[192,768]{1,0:T(8,128)}, u32[]{:S(2)}) copy-start(f32[192,768]{1,0:T(8,128)} %get-tuple-element.24) | copy-start | bytes 1769476

commit v4 on v3

--- a/solution.py
+++ b/solution.py
@@ -49,7 +49,7 @@
     attn_ref, dq_ref, dk_ref, dv_ref, gw_ref,
     wfull, ogown, ogcols, kvsend, kvext, gsend, grecv, prob, dmixed, mixed, mixall, acc, gpart, bias_ref, gwsend, gwrecv,
     local_sem, halo_s, halo_r, grad_s, grad_r, mix_s, mix_r,
-    wr_s, wr_r, wl_s, wl_r, wc_s, wc_r, wx_s, wx_r, wf_s, wf_r, og_s, og_r, gw_s, gw_r,
+    wr_s, wr_r, wl_s, wl_r, wc_s, wc_r, og_s, og_r, gw_s, gw_r,
 ):
     nt, nh, frames, rows, columns = dims
     t, h = lax.axis_index("tm"), lax.axis_index("height")
@@ -57,7 +57,7 @@
     model = og_hbm.shape[1]
     share = w_hbm.shape[0]
     heads = width // HEAD_DIM
-    quarter = model // 4
+    half = model // 2
     window = gpart.shape[1]
     span_cols = model // nt
     scale = 1.0 / math.sqrt(HEAD_DIM)
@@ -146,14 +146,7 @@
     steps = nh // 2
     core = lax.rem(t, 2)
     partner = (t + 1 - 2 * core, h)
-    pair = lax.rem(t // 2, 2)
-    across = (t + 2 - 4 * pair, h)
-
-    def quarter_of(i):
-        return pl.ds(pl.multiple_of(i * quarter, 128), quarter)
-
-    mine = quarter_of(2 * pair + core)
-    theirs = quarter_of(2 * (1 - pair) + core)
+    mine = pl.ds(pl.multiple_of(core * half, 128), half)
 
     def span(step, size, side):
         if step < steps - 1:
@@ -208,21 +201,9 @@
             lo, n = span(step, share, side)
             ref = wfull.at[wrow(at(pos + sign * (step + 1)), lo, n), mine]
             i = 2 * step + side
-            out.append(remote(ref, ref, wx_s.at[i], wx_r.at[i], across))
             out.append(remote(ref, ref, wc_s.at[i], wc_r.at[i], partner))
         for copy in out:
             copy.start()
-        return out
-
-    def pass_on(step):
-        out = []
-        for side, sign in enumerate((-1, 1)):
-            lo, n = span(step, share, side)
-            ref = wfull.at[wrow(at(pos + sign * (step + 1)), lo, n), theirs]
-            i = 2 * step + side
-            copy = remote(ref, ref, wf_s.at[i], wf_r.at[i], partner)
-            copy.start()
-            out.append(copy)
         return out
 
     own_w.wait()
@@ -249,11 +230,17 @@
         copy.start()
         gathers.append(copy)
     shared = []
-    for step in range(steps):
+
+    def w_step(step):
         for copy in live:
             copy.wait()
-        live = w_sends(step + 1) if step < steps - 1 else []
-        shared.append(share_sends(step))
+        live.clear()
+        if step < steps - 1:
+            live.extend(w_sends(step + 1))
+        shared.extend(share_sends(step))
+
+    for step in range(2):
+        w_step(step)
     exchange(halos, -1, "wait")
 
     group = 3 if heads % 3 == 0 else 1
@@ -299,11 +286,8 @@
         if step < steps:
             live.extend(gw_sends(step))
 
-    passed = []
-    for step in range(steps):
-        for copy in shared[step]:
-            copy.wait()
-        passed += pass_on(step)
+    for step in range(2, steps):
+        w_step(step)
 
     for copy in gathers:
         copy.wait()
@@ -315,7 +299,7 @@
 
     lax.fori_loop(0, width // 256, weight, 0)
     gw_step(0)
-    for copy in passed:
+    for copy in shared:
         copy.wait()
 
     def project(i, carry):
@@ -435,7 +419,6 @@
             dma((2,)), dma((8,)), dma((8,)), dma((8,)), dma((8,)),
             dma((nt - 1,)), dma((nt - 1,)),
             dma((steps,)), dma((steps,)), dma((steps,)), dma((steps,)),
-            dma((2 * steps,)), dma((2 * steps,)), dma((2 * steps,)), dma((2 * steps,)),
             dma((2 * steps,)), dma((2 * steps,)),
             dma((nt - 1,)), dma((nt - 1,)), dma((2 * steps,)), dma((2 * steps,)),
         ],

time: 153 us -> 133 us (0.87)
  Pallas kernels: 139 us -> 119 us
    pallas_call x1, Pallas kernels: 139 us -> 119 us  [shards(): pl.pallas_call(functools.partial(kernel, (nt, nh, frames, rows, columns))...]
where the time goes in v4:
time: 133 us
  Pallas kernels  119 us (89%)
  local copies, waits for them, and re-layouts  12.9 us (10%)
    pallas_call x1, Pallas kernels, shards(): pl.pallas_call(functools.partial(kernel, (nt, nh, frames, rows, columns))...  119 us

profile of v4, /device:TPU:0, one launch (start us, length us, event | category | flops | bytes accessed | tf_op | source)
XLA Modules:
  0.0 132.6 jit_solution(14923990904409267865)
XLA Ops:
  0.6 0.0 copy-start.2
  0.6 1.4 %copy.13.reach_ref = s32[4,8,2]{2,1,0:T(8,128)} copy(s32[4,8,2]{1,2,0:T(2,128)} %param.13) | data formatting | bytes 512 | tf_op args[5]
  2.1 0.0 copy-start
  2.1 1.9 %reshape.34.q_ref = bf16[128,1536]{1,0:T(8,128)(2,1)} reshape(bf16[4,8,4,1536]{3,2,1,0:T(4,128)(2,1)} %param.8) | data formatting | bytes 786432 | tf_op jit(solution)/shard_map/reshape | solution.py:429
  4.0 1.8 %reshape.35.k_ref = bf16[128,1536]{1,0:T(8,128)(2,1)} reshape(bf16[4,8,4,1536]{3,2,1,0:T(4,128)(2,1)} %param.9) | data formatting | bytes 786432 | tf_op jit(solution)/shard_map/reshape | solution.py:430
  5.8 0.0 copy-done.2
  5.8 0.8 reshape.36.v_ref
  6.7 0.0 copy-done
  6.7 1.1 reshape.37.og_hbm
  7.7 119.1 %shard_map.119 = (bf16[128,3072]{1,0:T(8,128)(2,1)}, bf16[128,1536]{1,0:T(8,128)(2,1)}, bf16[128,1536]{1,0:T(8,128)(2,1)}, bf16[128,1536]{1,0:T(8,128)(2,1)}, f32[192,768]{1,0:T(8,128)}) custom-call(bf16[128,1536]{1,0:T(8,128)(2,1)} %reshape.34.q_ref, bf16[128,1536]{1,0:T(8,128)(2,1)} %reshape.35.k_ref, bf16[128,1536]{1,0:T(8,128)(2,1)} %reshape.36.v_ref, ...), custom_call_target="tpu_custom_call" | custom-call | tf_op jit(solution)/shard_map/pallas_call | solution.py:391
  126.8 0.0 copy-start.5
  126.8 0.0 copy-start.4
  126.8 2.4 %reshape.38 = bf16[4,8,4,3072]{3,2,1,0:T(4,128)(2,1)} reshape(bf16[128,3072]{1,0:T(8,128)(2,1)} %get-tuple-element.10) | data formatting | bytes 1572864 | tf_op jit(solution)/shard_map/reshape | solution.py:445
  129.3 0.0 copy-done.5
  129.3 0.0 copy-start.3
  129.3 0.0 copy-start.1
  129.3 0.8 reshape.39
  130.1 0.0 copy-done.4
  130.1 0.8 reshape.40
  131.0 0.0 copy-done.3
  131.0 0.8 reshape.41
  131.8 0.0 copy-done.1
  131.8 0.8 copy.15
Async XLA Ops:
  0.6 5.2 %copy-start.2 = (bf16[4,8,4,1536]{3,2,1,0:T(4,128)(2,1)S(1)}, bf16[4,8,4,1536]{3,2,1,0:T(4,128)(2,1)}, u32[]{:S(2)}) copy-start(bf16[4,8,4,1536]{3,2,1,0:T(4,128)(2,1)} %param.10) | copy-start | bytes 1179652
  2.1 4.6 %copy-start = (bf16[4,8,4,3072]{3,2,1,0:T(4,128)(2,1)S(1)}, bf16[4,8,4,3072]{3,2,1,0:T(4,128)(2,1)}, u32[]{:S(2)}) copy-start(bf16[4,8,4,3072]{3,2,1,0:T(4,128)(2,1)} %param.12) | copy-start | bytes 2359300
  126.8 2.5 %copy-start.5 = (bf16[128,1536]{1,0:T(8,128)(2,1)S(1)}, bf16[128,1536]{1,0:T(8,128)(2,1)}, u32[]{:S(2)}) copy-start(bf16[128,1536]{1,0:T(8,128)(2,1)} %get-tuple-element.11) | copy-start | bytes 1179652
  126.8 3.3 %copy-start.4 = (bf16[128,1536]{1,0:T(8,128)(2,1)S(1)}, bf16[128,1536]{1,0:T(8,128)(2,1)}, u32[]{:S(2)}) copy-start(bf16[128,1536]{1,0:T(8,128)(2,1)} %get-tuple-element.12) | copy-start | bytes 1179652
  129.3 1.7 %copy-start.3 = (bf16[128,1536]{1,0:T(8,128)(2,1)S(1)}, bf16[128,1536]{1,0:T(8,128)(2,1)}, u32[]{:S(2)}) copy-start(bf16[128,1536]{1,0:T(8,128)(2,1)} %get-tuple-element.13) | copy-start | bytes 1179652
  129.3 2.5 %copy-start.1 = (f32[192,768]{1,0:T(8,128)S(1)}, f32[192,768]{1,0:T(8,128)}, u32[]{:S(2)}) copy-start(f32[192,768]{1,0:T(8,128)} %get-tuple-element.24) | copy-start | bytes 1769476
